TPU v7x, 128 devices: a whole 4x4x4 slice. The times are simulated.
128 devices in a mesh: dp: 8 (over z, core), seq: 16 (over x, y).
Axes of the slice: x: 4, y: 4, z: 4, core: 2. Of those that a mesh axis runs over, the one named last changes fastest.
Arguments:
- dec_input: bfloat16 [128, 128, 768], P(('dp', 'seq')), may hold values from -6 to 6
- memory: bfloat16 [128, 3072, 768], P('dp', 'seq'), may hold values from -6 to 6
- mem_len: int32 [128], P(('dp', 'seq')), may hold values from 1 to 3072, 196608 in all
- grad_out: bfloat16 [128, 128, 768], P(('dp', 'seq')), may hold values from -6 to 6
- attn_master: float32 [8, 768, 768], P(None, ('dp', 'seq'))
- ffn_in_master: float32 [2, 768, 2048], P(None, ('dp', 'seq')), may hold values from -0.21875 to 0.21875
- ffn_out_master: float32 [2048, 768], P(('dp', 'seq')), may hold values from -0.125 to 0.125
- gain_master: float32 [3, 768], P(None, ('dp', 'seq')), may hold values from 0.5 to 1.5
- attn_first: float32 [8, 768, 768], P(None, ('dp', 'seq')), may hold values from -64 to 64
- ffn_in_first: float32 [2, 768, 2048], P(None, ('dp', 'seq')), may hold values from -40 to 40
- ffn_out_first: float32 [2048, 768], P(('dp', 'seq')), may hold values from -40 to 40
- gain_first: float32 [3, 768], P(None, ('dp', 'seq')), may hold values from -96 to 96
- attn_second: float32 [8, 768, 768], P(None, ('dp', 'seq'))
- ffn_in_second: float32 [2, 768, 2048], P(None, ('dp', 'seq')), may hold values from 4.096 to 16.384
- ffn_out_second: float32 [2048, 768], P(('dp', 'seq')), may hold values from 4.096 to 16.384
- gain_second: float32 [3, 768], P(None, ('dp', 'seq'))
Outputs:
- out_block: bfloat16 [128, 128, 768], P(('dp', 'seq'))
- grad_input: float32 [128, 128, 768], P(('dp', 'seq'))
- grad_memory: float32 [128, 3072, 768], P('dp', 'seq')
- attn_new: float32 [8, 768, 768], P(None, ('dp', 'seq'))
- attn_first_new: float32 [8, 768, 768], P(None, ('dp', 'seq'))
- attn_second_new: float32 [8, 768, 768], P(None, ('dp', 'seq'))
- attn_copy: bfloat16 [8, 768, 768], P(None, ('dp', 'seq'))
- ffn_in_new: float32 [2, 768, 2048], P(None, ('dp', 'seq'))
- ffn_in_first_new: float32 [2, 768, 2048], P(None, ('dp', 'seq'))
- ffn_in_second_new: float32 [2, 768, 2048], P(None, ('dp', 'seq'))
- ffn_in_copy: bfloat16 [2, 768, 2048], P(None, ('dp', 'seq'))
- ffn_out_new: float32 [2048, 768], P(('dp', 'seq'))
- ffn_out_first_new: float32 [2048, 768], P(('dp', 'seq'))
- ffn_out_second_new: float32 [2048, 768], P(('dp', 'seq'))
- ffn_out_copy: bfloat16 [2048, 768], P(('dp', 'seq'))
- gain_new: float32 [3, 768], P(None, ('dp', 'seq'))
- gain_first_new: float32 [3, 768], P(None, ('dp', 'seq'))
- gain_second_new: float32 [3, 768], P(None, ('dp', 'seq'))
- gain_copy: bfloat16 [3, 768], P(None, ('dp', 'seq'))
Inputs may be any that keep to these rules, and one draw needn't show every extreme that they name: `mem_len`: each example's count of live memory positions; the largest is exactly 3072.
All inputs are finite; a program needn't handle non-finite values. No bound on the sum of `mem_len` on one device may be relied on, other than what follows from the above.
Results may differ from a plain program's by a relative error of at most 0.02.
The roundings to bfloat16 on the way count: a program that leaves them out, or rounds other values in their place, can miss the bound.
Values may be sent and summed in bfloat16 or wider, within the bound.
A program may use at most 256 MiB of HBM per device.

v0:
```python
import jax
import jax.numpy as jnp
from jax import lax
from jax.experimental import pallas as pl
from jax.experimental.pallas import tpu as pltpu
from jax.sharding import PartitionSpec as P

eps_norm = 1e-06
beta_one = 0.9
beta_two = 0.999
adam_eps = 1e-08
decay_rate = 0.01
rate_matrix = 0.12
rate_gain = 3.0
STEP = 10
MESH = pl.DeviceIdType.MESH
BF, F32 = jnp.bfloat16, jnp.float32
ALL = slice(None)
NEG = -1e30
PARTS_A = (("A", 0, "xyz"), ("A", 1, "yzx"), ("A", 2, "zxy"))
PARTS_F = (("B", 0, "xyz"), ("B", 1, "yxz"), ("C", 0, "xyz"))
PLANE = ("xy", "yx") * 3
PARTS_D = tuple(("D", n, PLANE[n]) for n in range(6))
AXES = {"A": "xyz", "B": "xyz", "C": "zxy", "D": "xy"}
STEPS = (2, -1, 1, 0)
VS = pl.BlockSpec(memory_space=pltpu.VMEM)
HS = pl.BlockSpec(memory_space=pltpu.HBM)
SDS = jax.ShapeDtypeStruct
DMA = pltpu.SemaphoreType.DMA


def vm(*shape):
    return pltpu.VMEM(shape, BF)


def vf(*shape):
    return pltpu.VMEM(shape, F32)


def where_am_i():
    dp, sq = lax.axis_index("dp"), lax.axis_index("seq")
    return {"x": sq // 4, "y": sq % 4, "z": dp // 2, "c": dp % 2}


def dev(at):
    return (at["z"] * 2 + at["c"], at["x"] * 4 + at["y"])


def moved(at, axis, step):
    return {**at, axis: (at[axis] + step + 4) % 4}


def offset(me, j, sign=1):
    return {**me, "x": (me["x"] + sign * (j // 4) + 4) % 4, "y": (me["y"] + sign * (j % 4) + 4) % 4}


def sibling_of(me):
    return {**me, "c": 1 - me["c"]}


def remote(src, dst, send, recv, to):
    return pltpu.make_async_remote_copy(src, dst, send, recv, device_id=dev(to), device_id_type=MESH)


def meet(me, column):
    dp, sq = lax.axis_index("dp"), lax.axis_index("seq")
    bar = pltpu.get_barrier_semaphore()
    for i in range(1, 16):
        pl.semaphore_signal(bar, inc=1, device_id=(dp, (sq + i) % 16), device_id_type=MESH)
    if column == "dp":
        for i in range(1, 8):
            pl.semaphore_signal(bar, inc=1, device_id=((dp + i) % 8, sq), device_id_type=MESH)
        return bar, 22
    if column == "z":
        for to in (moved(me, "z", 1), moved(me, "z", -1), sibling_of(me)):
            pl.semaphore_signal(bar, inc=1, device_id=dev(to), device_id_type=MESH)
        return bar, 18
    return bar, 15


def dot(a, b, ca=1, cb=0):
    return lax.dot_general(a, b, (((ca,), (cb,)), ((), ())), preferred_element_type=F32)


class Gather:
    def __init__(self, me, orders, view, own, ss, rs, sib_s=None, sib_r=None):
        self.me, self.orders, self.view, self.own = me, orders, view, own
        self.ss, self.rs, self.sib_s, self.sib_r = ss, rs, sib_s, sib_r
        self.count, self.last = len(orders), len(orders[0]) - 1

    def group(self, n, t, step, half=None):
        order = self.orders[n]
        at = moved(self.me, order[t], step)
        for j in range(t):
            at = {**at, order[j]: ALL}
        if half is not None and t:
            at = {**at, order[0]: pl.ds(2 * half, 2)}
        return at

    def kinds(self, n, t):
        return (0, 1, 2, 3) if t else (0, 1, 2 + n % 2)

    def copy(self, n, t, kind, back=0):
        axis = self.orders[n][t]
        step = 1 if kind in (0, 2) else -1
        dst = self.view(n, self.group(n, t, back) if kind < 2 else self.group(n, t, back - step, kind - 2))
        src = self.own(n) if t == 0 and kind < 2 and back == 0 else dst
        return remote(src, dst, self.ss.at[n, t, kind], self.rs.at[n, t, kind], moved(self.me, axis, step))

    def arrived(self, n, t, kind):
        self.copy(n, t, kind, -1 if kind in (0, 2) else 1).wait_recv()

    def sibling(self, n, j, c):
        v = self.view(n, {**self.group(n, self.last, (0, -1, 1, 2)[j]), "c": c})
        return remote(v, v, self.sib_s.at[n, j], self.sib_r.at[n, j], sibling_of(self.me))

    def send(self, t, ns=None):
        for n in ns or range(self.count):
            if t:
                for k in self.kinds(n, t - 1)[2:]:
                    self.arrived(n, t - 1, k)
            self.copy(n, t, 0).start()
            self.copy(n, t, 1).start()
            if self.sib_s is not None and t == self.last:
                self.sibling(n, 0, self.me["c"]).start()

    def forward(self, t, ns=None):
        for n in ns or range(self.count):
            for k in (0, 1):
                self.arrived(n, t, k)
                if 2 + k in self.kinds(n, t):
                    self.copy(n, t, 2 + k).start()
                if self.sib_s is not None and t == self.last:
                    self.sibling(n, 1 + k, self.me["c"]).start()

    def finish(self, ns=None):
        for n in ns or range(self.count):
            for k in (2, 3):
                self.arrived(n, self.last, k)
            if self.sib_s is not None:
                self.sibling(n, 3, self.me["c"]).start()

    def siblings_in(self):
        for n in range(self.count):
            for j in range(4):
                self.sibling(n, j, 1 - self.me["c"]).wait_recv()

    def drain(self):
        for n in range(self.count):
            for t in range(self.last + 1):
                for k in self.kinds(n, t):
                    self.copy(n, t, k).wait_send()
            if self.sib_s is not None:
                for j in range(4):
                    self.sibling(n, j, self.me["c"]).wait_send()


class Scatter:
    def __init__(self, me, parts, acc, hop, fin, ss, rs, sib=None, source=None, sib_s=None, sib_r=None, loc_s=None):
        self.me, self.parts, self.acc, self.hop_b, self.fin_b = me, parts, acc, hop, fin
        self.ss, self.rs, self.sib, self.source = ss, rs, sib, source
        self.sib_s, self.sib_r, self.loc_s = sib_s, sib_r, loc_s
        self.count, self.last = len(parts), len(parts[0][2]) - 1

    def idx(self, n, at):
        name, p, _ = self.parts[n]
        place = tuple(at[a] for a in AXES[name])
        return place if name == "C" else (p,) + place

    def slot(self, n):
        name, p, _ = self.parts[n]
        return () if name == "C" else (p,)

    def done(self, n, t):
        name, _, order = self.parts[n]
        return [a for a in AXES[name] if a in order[:t]]

    def group(self, n, t, step, half=None):
        order = self.parts[n][2]
        at = moved(self.me, order[t], step)
        for j in range(t):
            at = {**at, order[j]: ALL}
        if half is not None and t:
            at = {**at, self.done(n, t)[0]: pl.ds(2 * half, 2)}
        return at

    def kinds(self, n, t):
        return (0, 1) if t else (n % 2,)

    def refs(self, n, t):
        name = self.parts[n][0]
        return self.acc[name], self.hop_b[t][name], self.fin_b[t][name]

    def hop_copy(self, n, t, kind):
        step = 1 if kind == 0 else -1
        a, h, _ = self.refs(n, t)
        return remote(a.at[self.idx(n, self.group(n, t, 2 * step, kind))], h.at[self.slot(n) + (kind,)],
                      self.ss.at[n, t, kind], self.rs.at[n, t, kind], moved(self.me, self.parts[n][2][t], step))

    def fin_copy(self, n, t, kind):
        step = 1 if kind == 0 else -1
        a, _, f = self.refs(n, t)
        return remote(a.at[self.idx(n, self.group(n, t, step))], f.at[self.slot(n) + (kind,)],
                      self.ss.at[n, t, 2 + kind], self.rs.at[n, t, 2 + kind], moved(self.me, self.parts[n][2][t], step))

    def each(self, n, t, at, fn, half=None):
        axes = self.done(n, t)
        sizes, offs = [4] * len(axes), [0] * len(axes)
        if half is not None and axes:
            sizes[0], offs[0] = 2, 2 * half
        total = 1
        for s in sizes:
            total *= s

        def one(i):
            pos, rest = [], i
            for s in sizes[::-1]:
                pos.append(rest % s)
                rest = rest // s
            pos = pos[::-1]
            where = dict(at)
            for a, p, o in zip(axes, pos, offs):
                where[a] = p + o
            fn(self.idx(n, where), tuple(pos))

        if total == 1:
            one(0)
        else:
            pl.loop(0, total, unroll=4)(one)

    def sib_copy(self, n, j):
        at = self.group(n, self.last, STEPS[j])
        return remote(self.source(n, at, 1 - self.me["c"]), self.sib[self.parts[n][0]].at[self.idx(n, at)],
                      self.sib_s.at[n, j], self.sib_r.at[n, j], sibling_of(self.me))

    def loc_copy(self, n, j):
        at = self.group(n, self.last, STEPS[j])
        return pltpu.make_async_copy(self.source(n, at, self.me["c"]), self.acc[self.parts[n][0]].at[self.idx(n, at)], self.loc_s.at[n, j])

    def start(self):
        for j in range(4):
            for n in range(self.count):
                self.sib_copy(n, j).start()
                self.loc_copy(n, j).start()

    def merge(self, j):
        for n in range(self.count):
            self.sib_copy(n, j).wait_recv()
            self.loc_copy(n, j).wait()
            a, b = self.acc[self.parts[n][0]], self.sib[self.parts[n][0]]

            def fn(i, _):
                a[i] = (a[i].astype(F32) + b[i].astype(F32)).astype(BF)

            self.each(n, self.last, self.group(n, self.last, STEPS[j]), fn)

    def hop(self, t, ns=None):
        for n in ns or range(self.count):
            for k in self.kinds(n, t):
                self.hop_copy(n, t, k).start()

    def pass_on(self, t, ns=None):
        for n in ns or range(self.count):
            a, h, _ = self.refs(n, t)
            for k in (0, 1):
                if k in self.kinds(n, t):
                    self.hop_copy(n, t, k).wait_recv()

                    def fn(i, pos):
                        j = self.slot(n) + (k,) + pos
                        a[i] = (a[i].astype(F32) + h[j].astype(F32)).astype(BF)

                    self.each(n, t, self.group(n, t, 1 if k == 0 else -1), fn, k)
                self.fin_copy(n, t, k).start()

    def close(self, t, ns=None):
        for n in ns or range(self.count):
            self.fin_copy(n, t, 0).wait_recv()
            self.fin_copy(n, t, 1).wait_recv()
            a, _, f = self.refs(n, t)

            def fn(i, pos):
                s = self.slot(n)
                a[i] = (a[i].astype(F32) + f[s + (0,) + pos].astype(F32) + f[s + (1,) + pos].astype(F32)).astype(BF)

            self.each(n, t, self.group(n, t, 0), fn)

    def result(self, n):
        self.fin_copy(n, 0, 0).wait_recv()
        self.fin_copy(n, 0, 1).wait_recv()
        a, _, f = self.refs(n, 0)
        s = self.slot(n)
        return a[self.idx(n, self.me)].astype(F32) + f[s + (0,)].astype(F32) + f[s + (1,)].astype(F32)

    def drain(self):
        for n in range(self.count):
            if self.sib is not None:
                for j in range(4):
                    self.sib_copy(n, j).wait_send()
            for t in range(self.last + 1):
                for k in self.kinds(n, t):
                    self.hop_copy(n, t, k).wait_send()
                self.fin_copy(n, t, 0).wait_send()
                self.fin_copy(n, t, 1).wait_send()


def places(names, refs):
    return dict(zip(names, refs))


def stage_buffers(*shapes):
    out = []
    for lead in ((2, 2, 4), (2, 4, 4), (2, 2), (2, 4), (2,), (2,)):
        out += [vm(*pre, *lead, *block) for pre, block in shapes]
    return out


def staged(names, refs):
    k = len(names)
    got = [places(names, refs[k * i:k * i + k]) for i in range(6)]
    return {2: got[0], 1: got[2], 0: got[4]}, {2: got[1], 1: got[3], 0: got[5]}


def gather_kernel(attn, wi, wo, info, A, gains, lens, outB, outC, infos, stage, recv, blk, blkA, irecv,
                  ss, rs, sib_s, sib_r, as_, ar_, is_, ir_, ds_, dr_, own_s):
    me = where_am_i()
    dp, sq = lax.axis_index("dp"), lax.axis_index("seq")
    bar, count = meet(me, "dp")
    stage[:, 6:8, :] = jnp.zeros((16, 2, 640), F32)
    for s in range(16):
        stage[s, 0:6, 0:384] = attn[:, s // 2, 384 * (s % 2):384 * (s % 2) + 384]
        stage[s, 0:6, 384:640] = wi[:, s // 8, 256 * (s % 8):256 * (s % 8) + 256]
    pl.semaphore_wait(bar, count)

    def a2a(i):
        peer = (sq + i) % 16
        return pltpu.make_async_remote_copy(stage.at[peer], recv.at[sq], as_.at[i], ar_.at[i], device_id=(dp, peer), device_id_type=MESH)

    def inf(i):
        peer = (sq + i) % 16
        return pltpu.make_async_remote_copy(info, irecv.at[sq], is_.at[i], ir_.at[i], device_id=(dp, peer), device_id_type=MESH)

    for i in range(1, 16):
        a2a(i).start()
    for i in range(1, 16):
        inf(i).start()
    recv[sq] = stage[sq]
    irecv[sq] = info[...]
    outC[...] = wo[...].astype(BF)
    for i in range(1, 16):
        a2a(i).wait_recv()
    for k in range(16):
        blk[6 * k:6 * k + 6, :] = recv[k, 0:6, :]
    for p in range(3):
        blkA[p] = blk[32 * p:32 * p + 32, 0:384].astype(BF)
    for p in range(2):
        outB[p] = blk[48 * p:48 * p + 48, 384:640].astype(BF)
    place = lambda n, at: A.at[at["x"], at["y"], at["z"], at["c"], PARTS_A[n][1]]
    ring = Gather(me, [p[2] for p in PARTS_A], place, lambda n: blkA.at[n], ss, rs, sib_s, sib_r)
    owns = [pltpu.make_async_copy(blkA.at[n], place(n, me), own_s.at[n]) for n in range(3)]
    for o in owns:
        o.start()
    ring.send(0)
    ring.forward(0)
    for o in owns:
        o.wait()
    ring.send(1)
    ring.forward(1)
    ring.send(2)
    for i in range(1, 16):
        inf(i).wait_recv()
    tile = jnp.sum(irecv[...], axis=0)
    infos[dp] = tile

    def dpx(i, back=0):
        v = infos.at[(dp - back + 8) % 8]
        return pltpu.make_async_remote_copy(v, v, ds_.at[i], dr_.at[i], device_id=((dp + i) % 8, sq), device_id_type=MESH)

    for i in range(1, 8):
        dpx(i).start()
    ring.forward(2)
    for i in range(1, 8):
        dpx(i, i).wait_recv()
    lane = lax.broadcasted_iota(jnp.int32, (8, 128), 1)
    gains[...] = jnp.zeros((8, 768), F32)
    for d in range(8):
        lo, sh = 96 * d // 128, 96 * d % 128
        t = pltpu.roll(jnp.where(lane < 96, infos[d], 0.0), sh, 1)
        gains[:, 128 * lo:128 * lo + 128] += jnp.where(lane >= sh, t, 0.0)
        if sh > 32:
            gains[:, 128 * lo + 128:128 * lo + 256] += jnp.where(lane < sh, t, 0.0)
    pick = lax.broadcasted_iota(jnp.int32, (16, 128), 0) == lax.broadcasted_iota(jnp.int32, (16, 128), 1)
    lens[...] = jnp.broadcast_to(jnp.sum(jnp.where(pick, tile[3:4, :], 0.0), axis=1, keepdims=True), (16, 128))
    ring.finish()
    ring.siblings_in()
    for i in range(1, 16):
        a2a(i).wait_send()
        inf(i).wait_send()
    for i in range(1, 8):
        dpx(i).wait_send()
    ring.drain()


def gather(attn, wi, wo, info):
    return pl.pallas_call(
        gather_kernel,
        out_shape=(SDS((4, 4, 4, 2, 3, 32, 384), BF), SDS((8, 768), F32), SDS((16, 128), F32), SDS((2, 48, 256), BF), SDS((16, 768), BF)),
        in_specs=[VS] * 4, out_specs=(HS,) + (VS,) * 4,
        scratch_shapes=[vf(8, 8, 128), vf(16, 8, 640), vf(16, 8, 640), vf(96, 640), vm(3, 32, 384), vf(16, 8, 128),
                        DMA((3, 3, 4)), DMA((3, 3, 4)), DMA((3, 4)), DMA((3, 4)), DMA((16,)), DMA((16,)), DMA((16,)), DMA((16,)), DMA((8,)), DMA((8,)), DMA((3,))],
        compiler_params=pltpu.CompilerParams(collective_id=0, has_side_effects=True, vmem_limit_bytes=60 << 20),
        name="gather_attention_weights",
    )(attn, wi, wo, info)


def info_tile(gain, mem_len):
    sq = lax.axis_index("seq")
    t = jnp.zeros((8, 128), F32)
    t = lax.dynamic_update_slice(t, gain.astype(BF).astype(F32), (0, 6 * sq))
    return lax.dynamic_update_slice(t, mem_len.astype(F32)[:, None], (3, sq))


def scatter_kernel(GA, blkF, gg, oA, oB, oG, accA, sibA, h2, f2, h1, f1, h0, f0, blk, stage, recv, gdp, gsum, gsq,
                   ss, rs, sib_s, sib_r, loc_s, as_, ar_, is_, ir_, ds_, dr_):
    me = where_am_i()
    dp, sq = lax.axis_index("dp"), lax.axis_index("seq")
    bar, count = meet(me, "dp")
    pl.semaphore_wait(bar, count)
    hop, fin = staged("A", (h2, f2, h1, f1, h0, f0))
    ring = Scatter(me, PARTS_A, {"A": accA}, hop, fin, ss, rs, {"A": sibA},
                   lambda n, at, c: GA.at[at["x"], at["y"], at["z"], c, n], sib_s, sib_r, loc_s)
    ring.start()

    def dpx(i):
        peer = (dp + i) % 8
        return pltpu.make_async_remote_copy(gg.at[peer], gdp.at[dp], ds_.at[i], dr_.at[i], device_id=(peer, sq), device_id_type=MESH)

    for i in range(1, 8):
        dpx(i).start()
    gdp[dp] = gg[dp]
    ring.merge(0)
    ring.hop(2)
    ring.merge(1)
    ring.merge(2)
    ring.pass_on(2)
    ring.merge(3)
    for i in range(1, 8):
        dpx(i).wait_recv()
    gsum[...] = jnp.sum(gdp[...], axis=0)

    def inf(i):
        peer = (sq + i) % 16
        return pltpu.make_async_remote_copy(gsum, gsq.at[sq], is_.at[i], ir_.at[i], device_id=(dp, peer), device_id_type=MESH)

    for i in range(1, 16):
        inf(i).start()
    gsq[sq] = gsum[...]
    blk[:, 384:640] = blkF[...]
    stage[:, 6:8, :] = jnp.zeros((16, 2, 640), F32)
    ring.close(2)
    ring.hop(1)
    ring.pass_on(1)
    ring.close(1)
    ring.hop(0)
    ring.pass_on(0)
    for n in range(3):
        blk[32 * n:32 * n + 32, 0:384] = ring.result(n)
    for k in range(16):
        stage[k, 0:6, :] = blk[6 * k:6 * k + 6, :]

    def a2a(i):
        peer = (sq + i) % 16
        return pltpu.make_async_remote_copy(stage.at[peer], recv.at[sq], as_.at[i], ar_.at[i], device_id=(dp, peer), device_id_type=MESH)

    for i in range(1, 16):
        a2a(i).start()
    recv[sq] = stage[sq]
    for i in range(1, 16):
        inf(i).wait_recv()
    oG[...] = pltpu.roll(jnp.sum(gsq[...], axis=0), (128 - 6 * sq) % 128, 1)
    for i in range(1, 16):
        a2a(i).wait_recv()
    for s in range(16):
        oA[:, s // 2, 384 * (s % 2):384 * (s % 2) + 384] = recv[s, 0:6, 0:384]
        oB[:, s // 8, 256 * (s % 8):256 * (s % 8) + 256] = recv[s, 0:6, 384:640]
    for i in range(1, 8):
        dpx(i).wait_send()
    for i in range(1, 16):
        a2a(i).wait_send()
        inf(i).wait_send()
    ring.drain()


def scatter(GA, blkF, gg):
    return pl.pallas_call(
        scatter_kernel,
        out_shape=(SDS((6, 8, 768), F32), SDS((6, 2, 2048), F32), SDS((8, 128), F32)),
        in_specs=[HS, VS, VS], out_specs=(VS,) * 3,
        scratch_shapes=[vm(3, 4, 4, 4, 32, 384), vm(3, 4, 4, 4, 32, 384), *stage_buffers(((3,), (32, 384))),
                        vf(96, 640), vf(16, 8, 640), vf(16, 8, 640), vf(8, 8, 128), vf(8, 128), vf(16, 8, 128),
                        DMA((3, 3, 4)), DMA((3, 3, 4)), DMA((3, 4)), DMA((3, 4)), DMA((3, 4)),
                        DMA((16,)), DMA((16,)), DMA((16,)), DMA((16,)), DMA((8,)), DMA((8,))],
        compiler_params=pltpu.CompilerParams(collective_id=1, has_side_effects=True, vmem_limit_bytes=60 << 20),
        name="scatter_attention_grads",
    )(GA, blkF, gg)


def head_masks(value=1.0):
    lane = lax.broadcasted_iota(jnp.int32, (1, 256), 1)
    return [jnp.where(lane // 64 == h, value, 0.0).astype(BF) for h in range(4)]


def stack_heads(block, masks):
    return jnp.concatenate([block * m for m in masks], axis=0)


def key_positions():
    sq = lax.axis_index("seq")
    return (192 * sq + lax.broadcasted_iota(jnp.int32, (192, 128), 0)).astype(F32)


def ffn_place(B, C):
    def place(n, at):
        if n < 2:
            return B.at[at["x"], at["y"], at["z"], at["c"], n]
        return C.at[at["z"], at["c"], at["x"], at["y"]]
    return place


class Merge:
    def __init__(self, me, src, mid, one, two, ss, rs):
        self.me, self.src, self.mid, self.bufs, self.ss, self.rs = me, src, mid, (one, two), ss, rs

    def block(self, n, a, b):
        return (n, a, b) if n % 2 == 0 else (n, b, a)

    def copy(self, n, t, k):
        axis = PLANE[n][t]
        to = moved(self.me, axis, (1, -1, 2)[k])
        src = self.src.at[self.block(n, to[axis], ALL)] if t == 0 else self.mid.at[n, to[axis]]
        return remote(src, self.bufs[t].at[n, k], self.ss.at[n, t, k], self.rs.at[n, t, k], to)

    def send(self, t, ns):
        for n in ns:
            for k in (2, 0, 1):
                self.copy(n, t, k).start()

    def join(self, blocks):
        rows = [b[128:144, :].astype(F32)[0:8, :] for b in blocks]
        logs = [r + pltpu.roll(r, 6, 0) + pltpu.roll(r, 4, 0) for r in rows]
        top = logs[0]
        for l in logs[1:]:
            top = jnp.maximum(top, l)
        ws = [jnp.exp(l - top) for l in logs]
        total = ws[0] + ws[1] + ws[2] + ws[3]
        inv = 1.0 / total
        out = []
        for h in range(2):
            o = sum(b[64 * h:64 * h + 64, :].astype(F32) * (w * inv)[h:h + 1, :] for b, w in zip(blocks, ws))
            out.append(o)
        return jnp.concatenate(out, axis=0), top + jnp.log(total)

    def middle(self, ns):
        for n in ns:
            for k in range(3):
                self.copy(n, 0, k).wait_recv()
            a = self.me[PLANE[n][0]]

            for b in range(4):
                o, l = self.join([self.src.at[self.block(n, a, b)]] + [self.bufs[0].at[n, k, b] for k in range(3)])
                self.mid[n, b, 0:128, :] = o.astype(BF)
                self.mid[n, b, 128:144, :] = log_tile(l)

    def result(self, n):
        for k in range(3):
            self.copy(n, 1, k).wait_recv()
        return self.join([self.mid.at[n, self.me[PLANE[n][1]]]] + [self.bufs[1].at[n, k] for k in range(3)])

    def drain(self):
        for n in range(6):
            for t in range(2):
                for k in range(3):
                    self.copy(n, t, k).wait_send()


def log_tile(l):
    l = jnp.where(lax.broadcasted_iota(jnp.int32, (8, 128), 0) < 2, l, 0.0)
    high = l.astype(BF).astype(F32)
    middle = (l - high).astype(BF).astype(F32)
    low = l - high - middle
    return jnp.concatenate([high + pltpu.roll(middle, 2, 0) + pltpu.roll(low, 4, 0), jnp.zeros((8, 128), F32)], axis=0).astype(BF)


def pair_of(ref, g, at):
    return jnp.concatenate([ref[2 * g, at["x"], at["y"]], ref[2 * g + 1, at["x"], at["y"]]], axis=1)


def cross_fwd_kernel(q, lens, blkB, blkC, mem_h, A, q_h, k_h, v_h, kt_h, B, C, o_ref, L_ref,
                     qall, mem, wk, wv, wkT, wvT, K, V, KT, VT, ost, mid, one, two, lrow,
                     mem_s, w_s, out_s, ss, rs, os_, or_, fs, fr, fsib_s, fsib_r, own_s):
    me = where_am_i()
    bar, count = meet(me, "z")

    def load_mem(e):
        return pltpu.make_async_copy(mem_h.at[e], mem.at[e], mem_s.at[e])

    loads = [pltpu.make_async_copy(A.at[10 + i], (wk if i < 2 else wv).at[:, pl.ds(384 * (i % 2), 384)], w_s.at[i]) for i in range(4)]
    for c in loads:
        c.start()

    @pl.loop(0, 16)
    def _(e):
        load_mem(e).start()

    for n in range(6):
        qall[n, me["x"], me["y"]] = q[:, 128 * n:128 * n + 128]
    place = ffn_place(B, C)
    mine = lambda n: blkB.at[n] if n < 2 else blkC
    owns = [pltpu.make_async_copy(mine(n), place(n, me), own_s.at[n]) for n in range(3)]
    for c in owns:
        c.start()
    lrow[...] = jnp.zeros((4, 2, 8, 128), F32)
    pl.semaphore_wait(bar, count)
    view = lambda n, at: qall.at[n, at["x"], at["y"]]
    plane = Gather(me, PLANE, view, lambda n: view(n, me), ss, rs)
    ring = Gather(me, [p[2] for p in PARTS_F], place, mine, fs, fr, fsib_s, fsib_r)
    fold = Merge(me, ost, mid, one, two, os_, or_)
    plane.send(0)
    ring.send(0)
    for c in loads:
        c.wait()
    for i in range(6):
        wvT[:, 128 * i:128 * i + 128] = wv[128 * i:128 * i + 128, :].T
    plane.forward(0)
    ring.forward(0)
    for c in owns:
        c.wait()

    def project(a, b):
        @pl.loop(a // 2, b // 2)
        def _(i):
            for e in (2 * i, 2 * i + 1):
                load_mem(e).wait()
            K[pl.ds(2 * i, 2)] = dot(mem[pl.ds(2 * i, 2)].reshape(384, 768), wk[...]).astype(BF).reshape(2, 192, 768)
            for e in (2 * i, 2 * i + 1):
                VT[e] = dot(wvT[...], mem[e], 1, 1).astype(BF)

    def project_more(a, b):
        @pl.loop(a // 2, b // 2)
        def _(i):
            V[pl.ds(2 * i, 2)] = dot(mem[pl.ds(2 * i, 2)].reshape(384, 768), wv[...]).astype(BF).reshape(2, 192, 768)
            for e in (2 * i, 2 * i + 1):
                KT[e] = dot(wkT[...], mem[e], 1, 1).astype(BF)

    plane.send(1, (0, 1))
    project(0, 4)
    plane.send(1, (2, 3))
    plane.send(1, (4, 5))
    ring.send(1)
    project(4, 10)
    plane.forward(1, (0, 1))
    plane.forward(1, (2, 3))
    project(10, 16)
    ring.forward(1)
    plane.forward(1, (4, 5))
    ring.send(2)
    masks = head_masks()
    pos = key_positions()

    def attend(g):
        cols = slice(256 * g, 256 * g + 256)

        @pl.loop(0, 4)
        def _(i):
            four = [(x, x * 4 + y, {"x": x, "y": y}) for x, y in [(i, y) for y in range(4)]]
            sT = [dot(K[e, :, cols], stack_heads(pair_of(qall, g, at), masks), 1, 1) for _, e, at in four]
            pT, inv = [], []
            for u, (_, e, at) in enumerate(four):
                live = pos < lens[pl.ds(e, 1), :]
                ps = []
                for h in range(4):
                    s = jnp.where(live, sT[u][:, 128 * h:128 * h + 128], NEG)
                    top = jnp.max(s, axis=0, keepdims=True)
                    p = jnp.exp(s - top)
                    tot = jnp.sum(p, axis=0, keepdims=True)
                    lrow[u, h // 2, h % 2:h % 2 + 1, :] = top + jnp.log(tot)
                    ps.append(p.astype(BF))
                    inv.append(1.0 / tot)
                pT.append(jnp.concatenate(ps, axis=1))
            oT = [dot(VT[e, cols, :], p) for (_, e, _), p in zip(four, pT)]
            for u, (_, e, at) in enumerate(four):
                for h in range(4):
                    ost[2 * g + h // 2, at["x"], at["y"], 64 * (h % 2):64 * (h % 2) + 64, :] = (
                        oT[u][64 * h:64 * h + 64, 128 * h:128 * h + 128] * inv[4 * u + h]).astype(BF)
                for h in range(2):
                    ost[2 * g + h, at["x"], at["y"], 128:144, :] = log_tile(lrow[u, h])

        fold.send(0, (2 * g, 2 * g + 1))

    def deliver(g):
        for n in (2 * g, 2 * g + 1):
            o, l = fold.result(n)
            o_ref[:, 128 * n:128 * n + 128] = o.T
            L_ref[2 * n:2 * n + 2, :] = l[0:2, :]

    plane.finish((0, 1))
    attend(0)
    plane.finish((2, 3))
    attend(1)
    fold.middle((0, 1))
    fold.send(1, (0, 1))
    plane.finish((4, 5))
    out_q = pltpu.make_async_copy(qall, q_h, out_s.at[0])
    out_k = pltpu.make_async_copy(K, k_h, out_s.at[1])
    out_q.start()
    out_k.start()
    attend(2)
    ring.forward(2)
    fold.middle((2, 3))
    fold.send(1, (2, 3))
    for i in range(6):
        wkT[:, 128 * i:128 * i + 128] = wk[128 * i:128 * i + 128, :].T
    project_more(0, 8)
    fold.middle((4, 5))
    fold.send(1, (4, 5))
    low, high = pl.ds(0, 8), pl.ds(8, 8)
    outs = [pltpu.make_async_copy(a.at[k], b.at[k], out_s.at[2 + 2 * i + j])
            for j, k in enumerate((low, high)) for i, (a, b) in enumerate(((V, v_h), (KT, kt_h)))]
    for c in outs[:2]:
        c.start()
    ring.finish()
    project_more(8, 16)
    for c in outs[2:]:
        c.start()
    L_ref[12:16, :] = jnp.zeros((4, 128), F32)
    for g in range(3):
        deliver(g)
    plane.drain()
    fold.drain()
    for c in [out_q, out_k] + outs:
        c.wait()
    ring.siblings_in()
    ring.drain()


def cross_fwd(q, lens, blkB, blkC, memory, A):
    return pl.pallas_call(
        cross_fwd_kernel,
        out_shape=(SDS((6, 4, 4, 128, 128), BF), SDS((16, 192, 768), BF), SDS((16, 192, 768), BF), SDS((16, 768, 192), BF),
                   SDS((4, 4, 4, 2, 2, 48, 256), BF), SDS((4, 2, 4, 4, 16, 768), BF), SDS((128, 768), F32), SDS((16, 128), F32)),
        in_specs=[VS] * 4 + [HS] * 2, out_specs=(HS,) * 6 + (VS,) * 2,
        scratch_shapes=[vm(6, 4, 4, 128, 128), vm(16, 192, 768), vm(768, 768), vm(768, 768), vm(768, 768), vm(768, 768),
                        vm(16, 192, 768), vm(16, 192, 768), vm(16, 768, 192), vm(16, 768, 192),
                        vm(6, 4, 4, 144, 128), vm(6, 4, 144, 128), vm(6, 3, 4, 144, 128), vm(6, 3, 144, 128), vf(4, 2, 8, 128),
                        DMA((16,)), DMA((4,)), DMA((6,)), DMA((6, 2, 4)), DMA((6, 2, 4)), DMA((6, 2, 3)), DMA((6, 2, 3)),
                        DMA((3, 3, 4)), DMA((3, 3, 4)), DMA((3, 4)), DMA((3, 4)), DMA((3,))],
        compiler_params=pltpu.CompilerParams(collective_id=2, has_side_effects=True, vmem_limit_bytes=60 << 20),
        name="cross_forward",
    )(q, lens, blkB, blkC, memory, A)


def cross_bwd_kernel(do, st, lens, q_h, k_h, v_h, kt_h, mem_h, A, GB, GC, G_in, dq_ref, fB, fC, gm_h, dw_h,
                     qall, doall, stall, wk, wv, K, V, KT, mem, memT, dK, dV, gst, wst, dst, dh1, df1, dh0, df0,
                     accB, accC, sibB, sibC, hB2, hC2, fB2, fC2, hB1, hC1, fB1, fC1, hB0, hC0, fB0, fC0,
                     q_s, kv_s, mem_s, w_s, gm_s, dw_s, ss, rs, ds_, dr_, fs, fr, fsib_s, fsib_r, floc):
    me = where_am_i()
    bar, count = meet(me, "z")

    def load_mem(e):
        return pltpu.make_async_copy(mem_h.at[pl.ds(pl.multiple_of(256 * e, 256), 256)], mem.at[e % 4], mem_s.at[e % 4])

    for e in range(4):
        load_mem(e).start()
    loads = [pltpu.make_async_copy(A.at[10 + i], (wk if i < 2 else wv).at[:, pl.ds(384 * (i % 2), 384)], w_s.at[i]) for i in range(4)]
    loads.append(pltpu.make_async_copy(q_h, qall, q_s))
    for n in range(6):
        doall[n, me["x"], me["y"]] = do[:, 128 * n:128 * n + 128]
    stall[me["x"], me["y"]] = st[...]
    pl.semaphore_wait(bar, count)

    def place(n, at):
        return stall.at[at["x"], at["y"]] if n == 6 else doall.at[n, at["x"], at["y"]]

    plane = Gather(me, PLANE + ("xy",), place, lambda n: place(n, me), ss, rs)
    fhop, ffin = staged("BC", (hB2, hC2, fB2, fC2, hB1, hC1, fB1, fC1, hB0, hC0, fB0, fC0))
    grads = ffn_place(GB, GC)
    ring = Scatter(me, PARTS_F, {"B": accB, "C": accC}, fhop, ffin, fs, fr, {"B": sibB, "C": sibC},
                   lambda n, at, c: grads(n, {**at, "c": c}), fsib_s, fsib_r, floc)
    back = Scatter(me, PARTS_D, {"D": dst}, {1: {"D": dh1}, 0: {"D": dh0}}, {1: {"D": df1}, 0: {"D": df0}}, ds_, dr_)
    plane.send(0, (6, 0, 1, 2, 3, 4, 5))
    ring.start()
    for c in loads:
        c.start()

    def turn(a, b):
        @pl.loop(a, b)
        def _(e):
            load_mem(e).wait()
            memT[:, pl.ds(pl.multiple_of(256 * e, 256), 256)] = mem[e % 4].T

            @pl.when(e < 8)
            def _():
                load_mem(e + 4).start()

    turn(0, 1)
    plane.forward(0, (6, 0, 1, 2, 3, 4, 5))
    turn(1, 3)
    plane.send(1, (6, 0, 1))
    plane.send(1, (2, 3))
    plane.send(1, (4, 5))
    ring.merge(0)
    ring.hop(2)
    turn(3, 6)
    plane.forward(1, (6, 0, 1))
    ring.merge(1)
    ring.merge(2)
    plane.forward(1, (2, 3))
    ring.pass_on(2)
    masks = head_masks()
    pos = key_positions()

    def load_kv(g, i, u, which):
        e = ((me["x"] + 2 + i) % 4) * 4 + u
        cols = pl.ds(256 * g, 256)
        src = (k_h.at[e, :, cols], v_h.at[e, :, cols], kt_h.at[e, cols])[which]
        return pltpu.make_async_copy(src, (K, V, KT)[which].at[i % 2, u], kv_s.at[which, i % 2, u])

    def fetch_kv(g, i):
        for u in range(4):
            for w in range(3):
                load_kv(g, i, u, w).start()

    fetch_kv(0, 0)
    for c in loads:
        c.wait()

    def attend(g):
        cols = slice(256 * g, 256 * g + 256)

        @pl.loop(0, 4)
        def _(i):
            @pl.when(i < 3)
            def _():
                fetch_kv(g, i + 1)

            for u in range(4):
                for w in range(3):
                    load_kv(g, i, u, w).wait()
            x = (me["x"] + 2 + i) % 4
            four = [(x * 4 + y, {"x": x, "y": y}) for y in range(4)]
            q4s = [stack_heads(pair_of(qall, g, at), masks) for _, at in four]
            d4s = [stack_heads(pair_of(doall, g, at), masks) for _, at in four]
            sT = [dot(K[i % 2, u], q4s[u], 1, 1) for u in range(4)]
            gT = [dot(V[i % 2, u], d4s[u], 1, 1) for u in range(4)]
            pT, sg = [], []
            for u, (e, at) in enumerate(four):
                live = pos < lens[pl.ds(e, 1), :]
                ps, gs = [], []
                for h in range(4):
                    n = 4 * g + h
                    s = jnp.where(live, sT[u][:, 128 * h:128 * h + 128], NEG)
                    p = jnp.exp(s - stall[at["x"], at["y"], n:n + 1, :])
                    ps.append(p.astype(BF))
                    gs.append((p * (gT[u][:, 128 * h:128 * h + 128] - stall[at["x"], at["y"], 12 + n:13 + n, :])).astype(BF))
                pT.append(jnp.concatenate(ps, axis=1))
                sg.append(jnp.concatenate(gs, axis=1))
            for u, (e, at) in enumerate(four):
                dV[pl.ds(pl.multiple_of(192 * e, 192), 192), cols] = dot(pT[u], d4s[u]).astype(BF)
            for u, (e, at) in enumerate(four):
                dK[pl.ds(pl.multiple_of(192 * e, 192), 192), cols] = dot(sg[u], q4s[u]).astype(BF)
            for u, (e, at) in enumerate(four):
                qT = dot(KT[i % 2, u], sg[u])
                for h in range(4):
                    dst[2 * g + h // 2, at["x"], at["y"], 64 * (h % 2):64 * (h % 2) + 64, :] = qT[64 * h:64 * h + 64, 128 * h:128 * h + 128].astype(BF)

        if g < 2:
            fetch_kv(g + 1, 0)
        back.hop(1, (2 * g, 2 * g + 1))

    plane.finish((6, 0, 1))
    attend(0)
    plane.forward(1, (4, 5))
    plane.finish((2, 3))
    attend(1)
    back.pass_on(1, (0, 1))
    ring.merge(3)
    plane.finish((4, 5))
    attend(2)
    back.pass_on(1, (2, 3))
    back.close(1, (0, 1))
    back.hop(0, (0, 1))

    def gm_copy(e):
        return pltpu.make_async_copy(gst.at[e % 2], gm_h.at[e], gm_s.at[e % 2])

    def mem_grad(a, b):
        @pl.loop(a, b)
        def _(e):
            @pl.when(e > 1)
            def _():
                gm_copy(e - 2).wait()

            rows = pl.ds(pl.multiple_of(384 * e, 384), 384)
            gst[e % 2] = dot(dK[rows, :], wk[...], 1, 1) + dot(dV[rows, :], wv[...], 1, 1)
            gm_copy(e).start()

    def dw_copy(k, r, half):
        rows = pl.ds(pl.multiple_of(256 * r, 256), 256)
        return pltpu.make_async_copy(wst.at[k, :, pl.ds(384 * half, 384)], dw_h.at[10 + 2 * k + half, rows], dw_s.at[k, half])

    def weight_grad(a, b):
        @pl.loop(a, b)
        def _(r):
            for k in range(2):
                @pl.when(r > 0)
                def _():
                    dw_copy(k, r - 1, 0).wait()
                    dw_copy(k, r - 1, 1).wait()

                wst[k] = dot(memT[pl.ds(pl.multiple_of(256 * r, 256), 256), :], (dV if k else dK)[...]).astype(BF)
                dw_copy(k, r, 0).start()
                dw_copy(k, r, 1).start()

    turn(6, 12)
    ring.close(2)
    ring.hop(1)
    back.pass_on(1, (4, 5))
    back.close(1, (2, 3))
    back.hop(0, (2, 3))
    back.pass_on(0, (0, 1))
    mem_grad(0, 4)
    back.close(1, (4, 5))
    back.hop(0, (4, 5))
    back.pass_on(0, (2, 3))
    ring.pass_on(1)
    mem_grad(4, 8)
    back.pass_on(0, (4, 5))
    ring.close(1)
    ring.hop(0)
    weight_grad(0, 1)
    ring.pass_on(0)
    weight_grad(1, 3)
    for n in range(6):
        dq_ref[:, 128 * n:128 * n + 128] = (0.125 * back.result(n)).T
    fB[0:48, :] = ring.result(0)
    fB[48:96, :] = ring.result(1)
    fC[...] = ring.result(2)
    gm_copy(6).wait()
    gm_copy(7).wait()
    for k in range(2):
        dw_copy(k, 2, 0).wait()
        dw_copy(k, 2, 1).wait()
    plane.drain()
    ring.drain()
    back.drain()


def cross_bwd(do, st, lens, q_h, k_h, v_h, kt_h, memory, A, GB, GC, GA):
    bB, bC = (48, 256), (16, 768)
    return pl.pallas_call(
        cross_bwd_kernel,
        out_shape=(SDS((128, 768), F32), SDS((96, 256), F32), SDS((16, 768), F32), SDS((8, 384, 768), F32), SDS((16, 768, 384), BF)),
        in_specs=[VS] * 3 + [HS] * 9, out_specs=(VS,) * 3 + (HS,) * 2, input_output_aliases={11: 4},
        scratch_shapes=[vm(6, 4, 4, 128, 128), vm(6, 4, 4, 128, 128), vf(4, 4, 24, 128), vm(768, 768), vm(768, 768),
                        vm(2, 4, 192, 256), vm(2, 4, 192, 256), vm(2, 4, 256, 192), vm(4, 256, 768), vm(768, 3072), vm(3072, 768), vm(3072, 768),
                        vf(2, 384, 768), vm(2, 256, 768), vm(6, 4, 4, 128, 128), vm(6, 2, 2, 128, 128), vm(6, 2, 4, 128, 128), vm(6, 2, 128, 128), vm(6, 2, 128, 128),
                        vm(2, 4, 4, 4, *bB), vm(4, 4, 4, *bC), vm(2, 4, 4, 4, *bB), vm(4, 4, 4, *bC), *stage_buffers(((2,), bB), ((), bC)),
                        DMA, DMA((3, 2, 4)), DMA((4,)), DMA((4,)), DMA((2,)), DMA((2, 2)), DMA((7, 2, 4)), DMA((7, 2, 4)), DMA((6, 2, 4)), DMA((6, 2, 4)),
                        DMA((3, 3, 4)), DMA((3, 3, 4)), DMA((3, 4)), DMA((3, 4)), DMA((3, 4))],
        compiler_params=pltpu.CompilerParams(collective_id=3, has_side_effects=True, vmem_limit_bytes=60 << 20),
        name="cross_backward",
    )(do, st, lens, q_h, k_h, v_h, kt_h, memory.reshape(3072, 768), A, GB, GC, GA)


def adam_update(master, first, second, grad, rate):
    first_new = beta_one * first + (1.0 - beta_one) * grad
    second_new = beta_two * second + (1.0 - beta_two) * grad * grad
    fix_one = 1.0 - beta_one**STEP
    fix_two = 1.0 - beta_two**STEP
    master_new = master - rate * (
        first_new / fix_one / (jnp.sqrt(second_new / fix_two) + adam_eps) + decay_rate * master
    )
    return (master_new, first_new, second_new, master_new.astype(jnp.bfloat16))


def rms(x):
    return lax.rsqrt(jnp.mean(x * x, axis=-1, keepdims=True) + eps_norm)

def rms_back(x, inv, gain, u):
    scaled = u * gain
    inner = jnp.mean(scaled * x, axis=-1, keepdims=True)
    return inv * scaled - x * inv * inv * inv * inner, jnp.sum(u * x * inv, axis=0, keepdims=True)

def flip(x):
    return jnp.concatenate([x[:, 128 * i:128 * i + 128].T for i in range(x.shape[1] // 128)], axis=0)

def unflip(x):
    return jnp.concatenate([x[128 * i:128 * i + 128, :].T for i in range(x.shape[0] // 128)], axis=1)

def apply_w(h, W, k):
    return jnp.concatenate([dot(h, W[2 * k]), dot(h, W[2 * k + 1])], axis=1)

def apply_wt(u, W, k):
    return dot(u[:, 0:384], W[2 * k], 1, 1) + dot(u[:, 384:768], W[2 * k + 1], 1, 1)

def causal_mask():
    return lax.broadcasted_iota(jnp.int32, (128, 128), 0) <= lax.broadcasted_iota(jnp.int32, (128, 128), 1)

def self_fwd_kernel(x_ref, gains, A, q2, h1, qkv, o1, x1, h2, L1, W, sem):
    loads = [pltpu.make_async_copy(A.at[i], W.at[i], sem.at[i]) for i in range(10)]
    for c in loads:
        c.start()
    x = x_ref[...].astype(F32)
    h = (x * rms(x) * gains[0:1, :]).astype(BF)
    h1[...] = h
    for k in range(3):
        loads[2 * k].wait()
        loads[2 * k + 1].wait()
        full = apply_w(h, W, k)
        qkv[k] = full.astype(BF)
    vT = flip(full).astype(BF)
    masks = head_masks(0.125)
    live = causal_mask()
    outs = []
    for g in range(3):
        cols = slice(256 * g, 256 * g + 256)
        q4 = qkv[0, :, cols]
        sT = dot(qkv[1, :, cols], jnp.concatenate([q4 * m for m in masks], axis=0), 1, 1)
        ps = []
        for n in range(4):
            s = jnp.where(live, sT[:, 128 * n:128 * n + 128], NEG)
            top = jnp.max(s, axis=0, keepdims=True)
            lse = top + jnp.log(jnp.sum(jnp.exp(s - top), axis=0, keepdims=True))
            L1[4 * g + n:4 * g + n + 1, :] = lse
            ps.append(jnp.exp(s - lse).astype(BF))
        oT = dot(vT[256 * g:256 * g + 256, :], jnp.concatenate(ps, axis=1))
        outs += [oT[64 * n:64 * n + 64, 128 * n:128 * n + 128] for n in range(4)]
    o = unflip(jnp.concatenate(outs, axis=0)).astype(BF)
    o1[...] = o
    for c in loads[6:]:
        c.wait()
    x = x + apply_w(o, W, 3)
    x1[...] = x
    h = (x * rms(x) * gains[1:2, :]).astype(BF)
    h2[...] = h
    q2[...] = apply_w(h, W, 4).astype(BF) * jnp.asarray(0.125, BF)

def self_fwd(x, gains, A):
    row = SDS((128, 768), BF)
    return pl.pallas_call(
        self_fwd_kernel,
        out_shape=(row, row, SDS((3, 128, 768), BF), row, SDS((128, 768), F32), row, SDS((16, 128), F32)),
        in_specs=[VS, VS, HS], out_specs=(VS,) * 7,
        scratch_shapes=[pltpu.VMEM((10, 768, 384), BF), pltpu.SemaphoreType.DMA((10,))],
        compiler_params=pltpu.CompilerParams(vmem_limit_bytes=60 << 20),
        name="self_forward",
    )(x, gains, A)

def ffn_kernel(x1, o2, L2, dy_ref, gains, A, B, C, out, do2, st, dx2, gg, GA, GB, GC,
               W7, WB, WC, gA, gB, gC, sw, sb, sc, tb, tc, ta):
    lA = [pltpu.make_async_copy(A.at[14 + i], W7.at[i], sw.at[i]) for i in range(2)]
    lB = [pltpu.make_async_copy(B.at[i], WB.at[i], sb.at[i]) for i in range(16)]
    lC = [pltpu.make_async_copy(C.at[i], WC.at[i], sc.at[i]) for i in range(8)]
    for c in lA:
        c.start()
    for j in range(8):
        lB[j].start()
        lB[8 + j].start()
        lC[j].start()
    o = o2[...]
    ob = o.astype(BF)
    for c in lA:
        c.wait()
    x = x1[...] + apply_w(ob, W7, 0)
    inv = rms(x)
    h = (x * inv * gains[2:3, :]).astype(BF)
    hT = flip(h.astype(F32)).astype(BF)
    df = dy_ref[...]
    y = jnp.zeros((128, 768), F32)
    dh = jnp.zeros((128, 768), F32)
    c0 = 0.7978845608028654
    sB, sC = [], []
    for j in range(8):
        lB[j].wait()
        lB[8 + j].wait()
        lC[j].wait()
        a = dot(h, WB[j])
        up = dot(h, WB[8 + j])
        t = jnp.tanh(c0 * (a + 0.044715 * a * a * a))
        half = 0.5 * (1.0 + t)
        gel = a * half
        der = half + 0.5 * a * (1.0 - t * t) * (c0 * (1.0 + 0.134145 * a * a))
        mid32 = gel * up
        mid = mid32.astype(BF)
        y += dot(mid, WC[j])
        dm = dot(df, WC[j], 1, 1)
        dga = (dm * up * der).astype(BF)
        dup = (dm * gel).astype(BF)
        dh += dot(dga, WB[j], 1, 1) + dot(dup, WB[8 + j], 1, 1)
        gB[j] = dot(hT, dga).astype(BF)
        gB[8 + j] = dot(hT, dup).astype(BF)
        gC[j] = dot(flip(mid32).astype(BF), df).astype(BF)
        sB += [pltpu.make_async_copy(gB.at[j], GB.at[j], tb.at[j]), pltpu.make_async_copy(gB.at[8 + j], GB.at[8 + j], tb.at[8 + j])]
        sC += [pltpu.make_async_copy(gC.at[j], GC.at[j], tc.at[j])]
        for c in sB[-2:] + sC[-1:]:
            c.start()
    out[...] = (x + y).astype(BF)
    dz, gain = rms_back(x, inv, gains[2:3, :], dh)
    gg[...] = gain
    d = df.astype(F32) + dz
    dx2[...] = d
    dc = d.astype(BF)
    dof = apply_wt(dc, W7, 0).astype(BF)
    do2[...] = dof
    prod = flip(dof.astype(F32) * o)
    st[0:12, :] = L2[0:12, :]
    for n in range(12):
        st[12 + n:13 + n, :] = jnp.sum(prod[64 * n:64 * n + 64, :], axis=0, keepdims=True)
    oT = flip(o).astype(BF)
    sA = []
    for i in range(2):
        gA[i] = dot(oT, dc[:, 384 * i:384 * i + 384]).astype(BF)
        sA.append(pltpu.make_async_copy(gA.at[i], GA.at[14 + i], ta.at[i]))
        sA[-1].start()
    for c in sA + sB + sC:
        c.wait()

def ffn(x1, o2, L2, dy, gains, A, B, C):
    M = lambda *s: pltpu.VMEM(s, BF)
    D = pltpu.SemaphoreType.DMA
    return pl.pallas_call(
        ffn_kernel,
        out_shape=(SDS((128, 768), BF), SDS((128, 768), BF), SDS((24, 128), F32), SDS((128, 768), F32), SDS((1, 768), F32),
                   SDS((16, 768, 384), BF), SDS((16, 768, 256), BF), SDS((8, 256, 768), BF)),
        in_specs=[VS] * 5 + [HS] * 3, out_specs=(VS,) * 5 + (HS,) * 3,
        scratch_shapes=[M(2, 768, 384), M(16, 768, 256), M(8, 256, 768), M(2, 768, 384), M(16, 768, 256), M(8, 256, 768),
                        D((2,)), D((16,)), D((8,)), D((16,)), D((8,)), D((2,))],
        compiler_params=pltpu.CompilerParams(vmem_limit_bytes=60 << 20),
        name="feed_forward",
    )(x1, o2, L2, dy, gains, A, B, C)

def self_bwd_kernel(dq2, h2, x1, dx2, qkv, o1, L1, x_ref, h1, gains, g3, A, GA_in, gm_in, gin, tile, GA, gm,
                    W, G, gb, gmv, sem, gsem, msem):
    loads = [pltpu.make_async_copy(A.at[i], W.at[i], sem.at[i]) for i in range(10)]
    for i in (8, 9, 6, 7, 0, 1, 2, 3, 4, 5):
        loads[i].start()
    def gm_load(e):
        return pltpu.make_async_copy(gm_in.at[e], gmv.at[e], msem.at[e])
    def gm_store(e):
        return pltpu.make_async_copy(gmv.at[e], gm.at[e], msem.at[16 + e])
    for e in range(16):
        gm_load(e).start()
    stores = []
    def weight_grad(k, left, inc):
        for i in range(2):
            n = 2 * k + i
            G[n] = dot(left, inc[:, 384 * i:384 * i + 384]).astype(BF)
            stores.append(pltpu.make_async_copy(G.at[n], GA.at[n], gsem.at[n]))
            stores[-1].start()
    dqb = dq2[...].astype(BF)
    for i in (8, 9, 6, 7):
        loads[i].wait()
    u = apply_wt(dqb, W, 4)
    x = x1[...]
    inv = rms(x)
    dz, gain = rms_back(x, inv, gains[1:2, :], u)
    gb[...] = jnp.zeros((8, 768), F32)
    gb[1:2, :] = gain
    gb[2:3, :] = g3[...]
    d1 = dx2[...] + dz
    da = d1.astype(BF)
    do1 = apply_wt(da, W, 3).astype(BF)
    weight_grad(4, flip(h2[...].astype(F32)).astype(BF), dqb)
    masks = head_masks(0.125)
    ones = head_masks(1.0)
    live = causal_mask()
    kT = flip(qkv[1].astype(F32)).astype(BF)
    qs, ks, vs = [], [], []
    for g in range(3):
        cols = slice(256 * g, 256 * g + 256)
        q4 = qkv[0, :, cols]
        d4 = do1[:, cols]
        q4s = jnp.concatenate([q4 * m for m in masks], axis=0)
        d4s = jnp.concatenate([d4 * m for m in ones], axis=0)
        sT = dot(qkv[1, :, cols], q4s, 1, 1)
        gT = dot(qkv[2, :, cols], d4s, 1, 1)
        ps, gs = [], []
        for n in range(4):
            s = jnp.where(live, sT[:, 128 * n:128 * n + 128], NEG)
            p = jnp.exp(s - L1[4 * g + n:4 * g + n + 1, :])
            gt = gT[:, 128 * n:128 * n + 128]
            ps.append(p.astype(BF))
            gs.append((p * (gt - jnp.sum(p * gt, axis=0, keepdims=True))).astype(BF))
        sg = jnp.concatenate(gs, axis=1)
        vs.append(dot(jnp.concatenate(ps, axis=1), d4s).astype(BF))
        ks.append(dot(sg, q4s).astype(BF))
        qT = dot(kT[256 * g:256 * g + 256, :], sg)
        qs += [qT[64 * n:64 * n + 64, 128 * n:128 * n + 128] for n in range(4)]
    for e in range(16):
        gm_load(e).wait()
        gm_store(e).start()
    inc = [(0.125 * unflip(jnp.concatenate(qs, axis=0))).astype(BF), jnp.concatenate(ks, axis=1), jnp.concatenate(vs, axis=1)]
    weight_grad(3, flip(o1[...].astype(F32)).astype(BF), da)
    for c in loads[:6]:
        c.wait()
    u = apply_wt(inc[0], W, 0) + apply_wt(inc[1], W, 1) + apply_wt(inc[2], W, 2)
    x = x_ref[...].astype(F32)
    inv = rms(x)
    dz, gain = rms_back(x, inv, gains[0:1, :], u)
    gb[0:1, :] = gain
    gin[...] = d1 + dz
    hT = flip(h1[...].astype(F32)).astype(BF)
    for k in range(3):
        weight_grad(k, hT, inc[k])
    lane = lax.broadcasted_iota(jnp.int32, (8, 128), 1)
    for d in range(8):
        lo, sh = 96 * d // 128, 96 * d % 128
        t = pltpu.roll(gb[:, 128 * lo:128 * lo + 128], (128 - sh) % 128, 1)
        if sh > 32:
            nxt = pltpu.roll(gb[:, 128 * lo + 128:128 * lo + 256], (128 - sh) % 128, 1)
            t = jnp.where(lane < 128 - sh, t, nxt)
        tile[d] = jnp.where(lane < 96, t, 0.0)
    for c in stores:
        c.wait()
    for e in range(16):
        gm_store(e).wait()

def self_bwd(dq2, h2, x1, dx2, qkv, o1, L1, x, h1, gains, g3, A, GA, gm):
    D = pltpu.SemaphoreType.DMA
    return pl.pallas_call(
        self_bwd_kernel,
        out_shape=(SDS((128, 768), F32), SDS((8, 8, 128), F32), SDS((16, 768, 384), BF), SDS((16, 192, 768), F32)),
        in_specs=[VS] * 11 + [HS] * 3, out_specs=(VS, VS, HS, HS),
        input_output_aliases={12: 2},
        scratch_shapes=[pltpu.VMEM((10, 768, 384), BF), pltpu.VMEM((10, 768, 384), BF), pltpu.VMEM((8, 768), F32), pltpu.VMEM((16, 192, 768), F32), D((10,)), D((10,)), D((32,))],
        compiler_params=pltpu.CompilerParams(vmem_limit_bytes=60 << 20),
        name="self_backward",
    )(dq2, h2, x1, dx2, qkv, o1, L1, x, h1, gains, g3, A, GA, gm)

def adam_kernel(*refs):
    ins, outs = refs[:16], refs[16:]
    for n in range(4):
        w, m, v, g = ins[4 * n:4 * n + 4]
        grad = g[0:3, 0:6] if n == 3 else g[...]
        for o, val in zip(outs[4 * n:4 * n + 4], adam_update(w[...], m[...], v[...], grad, rate_gain if n == 3 else rate_matrix)):
            o[...] = val

def adam(*args):
    shapes = []
    for n in range(4):
        s = args[4 * n].shape
        shapes += [SDS(s, F32)] * 3 + [SDS(s, BF)]
    return pl.pallas_call(adam_kernel, out_shape=tuple(shapes), in_specs=[VS] * 16, out_specs=(VS,) * 16,
                          compiler_params=pltpu.CompilerParams(vmem_limit_bytes=60 << 20), name="adam")(*args)


def body(
    dec_input,
    memory,
    mem_len,
    grad_out,
    attn_master,
    ffn_in_master,
    ffn_out_master,
    gain_master,
    attn_first,
    ffn_in_first,
    ffn_out_first,
    gain_first,
    attn_second,
    ffn_in_second,
    ffn_out_second,
    gain_second,
):
    swap = lambda a: a.transpose(1, 0, 2)
    attn_t, in_t = swap(attn_master), swap(ffn_in_master)
    gath_a, gains, lens, blk_b, blk_c = gather(attn_t, in_t, ffn_out_master, info_tile(gain_master, mem_len))
    aw = gath_a.reshape(16, 768, 384)
    x = dec_input[0]
    q2, h1, qkv, o1, x1, h2, L1 = self_fwd(x, gains, aw)
    q_all, k_two, v_two, kt_two, gath_b, gath_c, o2, L2 = cross_fwd(q2, lens, blk_b, blk_c, memory, aw)
    out_block, do2, st, dx2, g3, GA, GB, GC = ffn(x1, o2, L2, grad_out[0], gains, aw, gath_b.reshape(16, 768, 256), gath_c.reshape(8, 256, 768))
    dq2, blk_f, share_c, gm, GA = cross_bwd(
        do2, st, lens, q_all, k_two, v_two, kt_two, memory, aw,
        GB.reshape(4, 4, 4, 2, 2, 48, 256), GC.reshape(4, 2, 4, 4, 16, 768), GA,
    )
    grad_input, tile_g, GA, grad_memory = self_bwd(dq2, h2, x1, dx2, qkv, o1, L1, x, h1, gains, g3, aw, GA, gm.reshape(16, 192, 768))
    share_a, share_b, share_g = scatter(GA.reshape(4, 4, 4, 2, 3, 32, 384), blk_f, tile_g)
    new = adam(
        attn_t, swap(attn_first), swap(attn_second), share_a,
        in_t, swap(ffn_in_first), swap(ffn_in_second), share_b,
        ffn_out_master, ffn_out_first, ffn_out_second, share_c,
        gain_master, gain_first, gain_second, share_g,
    )
    return (out_block[None], grad_input[None], grad_memory, *[swap(a) for a in new[:8]], *new[8:])


def solution(mesh):
    placed = (
        P(("dp", "seq"), None, None),
        P("dp", "seq", None),
        P(("dp", "seq")),
        P(("dp", "seq"), None, None),
        P(None, ("dp", "seq"), None),
        P(None, ("dp", "seq"), None),
        P(("dp", "seq"), None),
        P(None, ("dp", "seq")),
        P(None, ("dp", "seq"), None),
        P(None, ("dp", "seq"), None),
        P(("dp", "seq"), None),
        P(None, ("dp", "seq")),
        P(None, ("dp", "seq"), None),
        P(None, ("dp", "seq"), None),
        P(("dp", "seq"), None),
        P(None, ("dp", "seq")),
    )
    return jax.shard_map(
        body,
        mesh=mesh,
        in_specs=placed,
        out_specs=(
            P(("dp", "seq"), None, None),
            P(("dp", "seq"), None, None),
            P("dp", "seq", None),
            P(None, ("dp", "seq"), None),
            P(None, ("dp", "seq"), None),
            P(None, ("dp", "seq"), None),
            P(None, ("dp", "seq"), None),
            P(None, ("dp", "seq"), None),
            P(None, ("dp", "seq"), None),
            P(None, ("dp", "seq"), None),
            P(None, ("dp", "seq"), None),
            P(("dp", "seq"), None),
            P(("dp", "seq"), None),
            P(("dp", "seq"), None),
            P(("dp", "seq"), None),
            P(None, ("dp", "seq")),
            P(None, ("dp", "seq")),
            P(None, ("dp", "seq")),
            P(None, ("dp", "seq")),
        ),
        check_vma=False,
    )
```

profile of v0, /device:TPU:0, one launch (start us, length us, event | category | flops | bytes accessed | tf_op | source)
XLA Modules:
  0.0 313.4 jit_solution(14921544821654613293)
XLA Ops:
  1.3 0.7 convert_convert_fusion
  2.0 0.2 dynamic_update_slice.6
  2.2 0.1 dynamic_update_slice.7.info
  2.3 0.0 copy-start
  2.3 0.6 copy-done
  2.9 51.8 %gather_attention_weights.1 = (bf16[4,4,4,2,3,32,384]{6,5,4,3,2,1,0:T(8,128)(2,1)}, f32[8,768]{1,0:T(8,128)}, f32[16,128]{1,0:T(8,128)}, bf16[2,48,256]{2,1,0:T(8,128)(2,1)}, bf16[16,768]{1,0:T(8,128)(2,1)}) custom-call(f32[6,8,768]{2,1,0:T(8,128)} %bitcast.41, f32[6,2,2048]{2,1,0:T(2,128)} %bitcast.43, f32[16,768]{1,0:T(8,128)} %refs_8_.1, f32[8,128]{1,0:T(8,128)} %copy-done), custom_call_target="tpu_custom_call" | custom-call | tf_op jit(solution)/shard_map/gather_attention_weights/pallas_call | solution.py:405
  54.7 5.9 %self_forward.1 = (bf16[128,768]{1,0:T(8,128)(2,1)}, bf16[128,768]{1,0:T(8,128)(2,1)}, bf16[3,128,768]{2,1,0:T(8,128)(2,1)}, bf16[128,768]{1,0:T(8,128)(2,1)}, f...) custom-call(bf16[128,768]{1,0:T(8,128)(2,1)} %bitcast.39, f32[8,768]{1,0:T(8,128)} %get-tuple-element.75.gains, ...), custom_call_target="tpu_custom_call" | custom-call | tf_op jit(solution)/shard_map/self_forward/pallas_call | solution.py:1050
  60.6 80.9 %cross_forward.1 = (bf16[6,4,4,128,128]{4,3,2,1,0:T(8,128)(2,1)}, bf16[16,192,768]{2,1,0:T(8,128)(2,1)}, bf16[16,192,768]{2,1,0:T(8,128)(2,1)}, bf16[16,768,192]...) custom-call(bf16[128,768]{1,0:T(8,128)(2,1)} %get-tuple-element.78.q, ...), custom_call_target="tpu_custom_call" | custom-call | tf_op jit(solution)/shard_map/cross_forward/pallas_call | solution.py:747
  141.6 19.3 %feed_forward.1 = (bf16[128,768]{1,0:T(8,128)(2,1)}, bf16[128,768]{1,0:T(8,128)(2,1)}, f32[24,128]{1,0:T(8,128)}, f32[128,768]{1,0:T(8,128)}, f32[1,768]{1,0:T(1...) custom-call(f32[128,768]{1,0:T(8,128)} %get-tuple-element.77.x1, ...), custom_call_target="tpu_custom_call" | custom-call | tf_op jit(solution)/shard_map/feed_forward/pallas_call | solution.py:1131
  160.9 86.3 %cross_backward.1 = (f32[128,768]{1,0:T(8,128)}, f32[96,256]{1,0:T(8,128)}, f32[16,768]{1,0:T(8,128)}, f32[8,384,768]{2,1,0:T(8,128)}, bf16[16,768,384]{2,1,0:T(8,128)(2,1)}) custom-call(bf16[128,768]{1,0:T(8,128)(2,1)} %get-tuple-element.87.do, f32[24,128]{1,0:T(8,128)} %get-tuple-element.88.st, ...), custom_call_target="tpu_custom_call", output_to_operand_aliasing={{4}: (11, {})} | custom-call | tf_op jit(solution)/shard_map/cross_backward/pallas_call | solution.py:960
  247.2 13.7 %self_backward.1 = (f32[128,768]{1,0:T(8,128)}, f32[8,8,128]{2,1,0:T(8,128)}, bf16[16,768,384]{2,1,0:T(8,128)(2,1)}, f32[16,192,768]{2,1,0:T(8,128)}) custom-call(f32[128,768]{1,0:T(8,128)} %get-tuple-element.96.dq2, bf16[128,768]{1,0:T(8,128)(2,1)} %get-tuple-element.97.h2, f32[128,768]{1,0:T(8,128)} %get-tuple-element.77.x1, ...), custom_call_target="tpu_custom_call", output_to_operand_aliasing={{2}: (12, {})} | custom-call | tf_op jit(solution)/shard_map/self_backward/pallas_call | solution.py:1230
  261.0 49.7 %scatter_attention_grads.1 = (f32[6,8,768]{2,1,0:T(8,128)}, f32[6,2,2048]{2,1,0:T(2,128)}, f32[8,128]{1,0:T(8,128)}) custom-call(bf16[4,4,4,2,3,32,384]{6,5,4,3,2,1,0:T(8,128)(2,1)} %bitcast.32, f32[96,256]{1,0:T(8,128)} %get-tuple-element.109.blkF, f32[8,8,128]{2,1,0:T(8,128)} %get-tuple-element.110.gg), custom_call_target="tpu_custom_call" | custom-call | tf_op jit(solution)/shard_map/scatter_attention_grads/pallas_call | solution.py:495
  310.7 2.5 adam.1
  (1 shorter events, 0.0 us)
Async XLA Ops:
  2.3 0.6 copy-start
where the time goes:
time: 318 us; the launch traced here: 313 us
  Pallas kernels  310 us (97%)
    pallas_call x1, Pallas kernels, cross_bwd(): pl.pallas_call(cross_bwd_kernel, out_shape=(SDS((128, 768), F32), SDS((96...  86.3 us
    pallas_call x1, Pallas kernels, cross_fwd(): pl.pallas_call(cross_fwd_kernel, out_shape=(SDS((6, 4, 4, 128, 128), BF),...  80.9 us
    pallas_call x1, Pallas kernels, gather(): pl.pallas_call(gather_kernel, out_shape=(SDS((4, 4, 4, 2, 3, 32, 384), BF...  51.8 us
    pallas_call x1, Pallas kernels, scatter(): pl.pallas_call(scatter_kernel, out_shape=(SDS((6, 8, 768), F32), SDS((6,...  49.7 us
    pallas_call x1, Pallas kernels, ffn(): pl.pallas_call(ffn_kernel, out_shape=(SDS((128, 768), BF), SDS((128, 768)...  19.3 us
    pallas_call x1, Pallas kernels, self_bwd(): pl.pallas_call(self_bwd_kernel, out_shape=(SDS((128, 768), F32), SDS((8,...  13.7 us

commit v1 on v0

--- a/solution.py
+++ b/solution.py
@@ -18,10 +18,11 @@
 ALL = slice(None)
 NEG = -1e30
 PARTS_A = (("A", 0, "xyz"), ("A", 1, "yzx"), ("A", 2, "zxy"))
-PARTS_F = (("B", 0, "xyz"), ("B", 1, "yxz"), ("C", 0, "xyz"))
+PARTS_F = (("B", 0, "z"), ("B", 1, "z"), ("C", 0, "z"))
+PARTS_G = (("E", 0, "xy"), ("E", 1, "yx"), ("F", 0, "xy"))
 PLANE = ("xy", "yx") * 3
 PARTS_D = tuple(("D", n, PLANE[n]) for n in range(6))
-AXES = {"A": "xyz", "B": "xyz", "C": "zxy", "D": "xy"}
+AXES = {"A": "xyz", "B": "xyz", "C": "zxy", "D": "xy", "E": "xy", "F": "xy"}
 STEPS = (2, -1, 1, 0)
 VS = pl.BlockSpec(memory_space=pltpu.VMEM)
 HS = pl.BlockSpec(memory_space=pltpu.HBM)
@@ -83,28 +84,26 @@
 
 
 class Gather:
-    def __init__(self, me, orders, view, own, ss, rs, sib_s=None, sib_r=None):
-        self.me, self.orders, self.view, self.own = me, orders, view, own
+    def __init__(self, me, orders, view, own, ss, rs, sib_s=None, sib_r=None, whole=""):
+        self.me, self.orders, self.view, self.own, self.whole = me, orders, view, own, whole
         self.ss, self.rs, self.sib_s, self.sib_r = ss, rs, sib_s, sib_r
         self.count, self.last = len(orders), len(orders[0]) - 1
 
     def group(self, n, t, step, half=None):
-        order = self.orders[n]
-        at = moved(self.me, order[t], step)
-        for j in range(t):
-            at = {**at, order[j]: ALL}
-        if half is not None and t:
-            at = {**at, order[0]: pl.ds(2 * half, 2)}
+        axes = self.whole + self.orders[n][:t]
+        at = {**moved(self.me, self.orders[n][t], step), **{a: ALL for a in axes}}
+        if half is not None and axes:
+            at[axes[0]] = pl.ds(2 * half, 2)
         return at
 
     def kinds(self, n, t):
-        return (0, 1, 2, 3) if t else (0, 1, 2 + n % 2)
+        return (0, 1, 2, 3) if t or self.whole else (0, 1, 2 + n % 2)
 
     def copy(self, n, t, kind, back=0):
         axis = self.orders[n][t]
         step = 1 if kind in (0, 2) else -1
         dst = self.view(n, self.group(n, t, back) if kind < 2 else self.group(n, t, back - step, kind - 2))
-        src = self.own(n) if t == 0 and kind < 2 and back == 0 else dst
+        src = self.own(n) if self.own and t == 0 and kind < 2 and back == 0 else dst
         return remote(src, dst, self.ss.at[n, t, kind], self.rs.at[n, t, kind], moved(self.me, axis, step))
 
     def arrived(self, n, t, kind):
@@ -156,7 +155,8 @@
 
 
 class Scatter:
-    def __init__(self, me, parts, acc, hop, fin, ss, rs, sib=None, source=None, sib_s=None, sib_r=None, loc_s=None):
+    def __init__(self, me, parts, acc, hop, fin, ss, rs, sib=None, source=None, sib_s=None, sib_r=None, loc_s=None, whole=""):
+        self.whole = whole
         self.me, self.parts, self.acc, self.hop_b, self.fin_b = me, parts, acc, hop, fin
         self.ss, self.rs, self.sib, self.source = ss, rs, sib, source
         self.sib_s, self.sib_r, self.loc_s = sib_s, sib_r, loc_s
@@ -165,27 +165,25 @@
     def idx(self, n, at):
         name, p, _ = self.parts[n]
         place = tuple(at[a] for a in AXES[name])
-        return place if name == "C" else (p,) + place
+        return place if name in "CF" else (p,) + place
 
     def slot(self, n):
         name, p, _ = self.parts[n]
-        return () if name == "C" else (p,)
+        return () if name in "CF" else (p,)
 
     def done(self, n, t):
         name, _, order = self.parts[n]
-        return [a for a in AXES[name] if a in order[:t]]
+        return [a for a in AXES[name] if a in self.whole + order[:t]]
 
     def group(self, n, t, step, half=None):
-        order = self.parts[n][2]
-        at = moved(self.me, order[t], step)
-        for j in range(t):
-            at = {**at, order[j]: ALL}
-        if half is not None and t:
-            at = {**at, self.done(n, t)[0]: pl.ds(2 * half, 2)}
+        axes = self.done(n, t)
+        at = {**moved(self.me, self.parts[n][2][t], step), **{a: ALL for a in axes}}
+        if half is not None and axes:
+            at[axes[0]] = pl.ds(2 * half, 2)
         return at
 
     def kinds(self, n, t):
-        return (0, 1) if t else (n % 2,)
+        return (0, 1) if t or self.whole else (n % 2,)
 
     def refs(self, n, t):
         name = self.parts[n][0]
@@ -304,25 +302,30 @@
                 self.fin_copy(n, t, 1).wait_send()
 
 
-def places(names, refs):
-    return dict(zip(names, refs))
-
-
-def stage_buffers(*shapes):
-    out = []
-    for lead in ((2, 2, 4), (2, 4, 4), (2, 2), (2, 4), (2,), (2,)):
-        out += [vm(*pre, *lead, *block) for pre, block in shapes]
-    return out
+def stage_buffers(leads, *shapes):
+    return [vm(*pre, *lead, *block) for lead in leads for pre, block in shapes]
+
+
+LEADS = ((2, 2, 4), (2, 4, 4), (2, 2), (2, 4), (2,), (2,))
 
 
 def staged(names, refs):
     k = len(names)
-    got = [places(names, refs[k * i:k * i + k]) for i in range(6)]
-    return {2: got[0], 1: got[2], 0: got[4]}, {2: got[1], 1: got[3], 0: got[5]}
-
-
-def gather_kernel(attn, wi, wo, info, A, gains, lens, outB, outC, infos, stage, recv, blk, blkA, irecv,
-                  ss, rs, sib_s, sib_r, as_, ar_, is_, ir_, ds_, dr_, own_s):
+    got = [dict(zip(names, refs[k * i:k * i + k])) for i in range(len(refs) // k)]
+    last = len(got) // 2 - 1
+    return {last - t: got[2 * t] for t in range(last + 1)}, {last - t: got[2 * t + 1] for t in range(last + 1)}
+
+
+def ffn_place(B, C):
+    def place(n, at):
+        if n < 2:
+            return B.at[at["x"], at["y"], at["z"], at["c"], n]
+        return C.at[at["z"], at["c"], at["x"], at["y"]]
+    return place
+
+
+def gather_kernel(attn, wi, wo, info, A, B, C, gains, lens, infos, stage, recv, blk, blkA, blkB, blkC, irecv,
+                  fs, fr, ss, rs, sib_s, sib_r, as_, ar_, is_, ir_, ds_, dr_, own_s):
     me = where_am_i()
     dp, sq = lax.axis_index("dp"), lax.axis_index("seq")
     bar, count = meet(me, "dp")
@@ -346,7 +349,7 @@
         inf(i).start()
     recv[sq] = stage[sq]
     irecv[sq] = info[...]
-    outC[...] = wo[...].astype(BF)
+    blkC[...] = wo[...].astype(BF)
     for i in range(1, 16):
         a2a(i).wait_recv()
     for k in range(16):
@@ -354,19 +357,27 @@
     for p in range(3):
         blkA[p] = blk[32 * p:32 * p + 32, 0:384].astype(BF)
     for p in range(2):
-        outB[p] = blk[48 * p:48 * p + 48, 384:640].astype(BF)
+        blkB[p] = blk[48 * p:48 * p + 48, 384:640].astype(BF)
     place = lambda n, at: A.at[at["x"], at["y"], at["z"], at["c"], PARTS_A[n][1]]
     ring = Gather(me, [p[2] for p in PARTS_A], place, lambda n: blkA.at[n], ss, rs, sib_s, sib_r)
+    place_f = ffn_place(B, C)
+    mine = lambda n: blkB.at[n] if n < 2 else blkC
+    ring_f = Gather(me, [p[2] for p in PARTS_G], place_f, mine, fs, fr)
     owns = [pltpu.make_async_copy(blkA.at[n], place(n, me), own_s.at[n]) for n in range(3)]
+    owns += [pltpu.make_async_copy(mine(n), place_f(n, me), own_s.at[3 + n]) for n in range(3)]
     for o in owns:
         o.start()
     ring.send(0)
+    ring_f.send(0)
     ring.forward(0)
+    ring_f.forward(0)
     for o in owns:
         o.wait()
     ring.send(1)
+    ring_f.send(1)
     ring.forward(1)
     ring.send(2)
+    ring_f.forward(1)
     for i in range(1, 16):
         inf(i).wait_recv()
     tile = jnp.sum(irecv[...], axis=0)
@@ -391,8 +402,10 @@
             gains[:, 128 * lo + 128:128 * lo + 256] += jnp.where(lane < sh, t, 0.0)
     pick = lax.broadcasted_iota(jnp.int32, (16, 128), 0) == lax.broadcasted_iota(jnp.int32, (16, 128), 1)
     lens[...] = jnp.broadcast_to(jnp.sum(jnp.where(pick, tile[3:4, :], 0.0), axis=1, keepdims=True), (16, 128))
+    ring_f.finish()
     ring.finish()
     ring.siblings_in()
+    ring_f.drain()
     for i in range(1, 16):
         a2a(i).wait_send()
         inf(i).wait_send()
@@ -404,10 +417,10 @@
 def gather(attn, wi, wo, info):
     return pl.pallas_call(
         gather_kernel,
-        out_shape=(SDS((4, 4, 4, 2, 3, 32, 384), BF), SDS((8, 768), F32), SDS((16, 128), F32), SDS((2, 48, 256), BF), SDS((16, 768), BF)),
-        in_specs=[VS] * 4, out_specs=(HS,) + (VS,) * 4,
-        scratch_shapes=[vf(8, 8, 128), vf(16, 8, 640), vf(16, 8, 640), vf(96, 640), vm(3, 32, 384), vf(16, 8, 128),
-                        DMA((3, 3, 4)), DMA((3, 3, 4)), DMA((3, 4)), DMA((3, 4)), DMA((16,)), DMA((16,)), DMA((16,)), DMA((16,)), DMA((8,)), DMA((8,)), DMA((3,))],
+        out_shape=(SDS((4, 4, 4, 2, 3, 32, 384), BF), SDS((4, 4, 4, 2, 2, 48, 256), BF), SDS((4, 2, 4, 4, 16, 768), BF), SDS((8, 768), F32), SDS((16, 128), F32)),
+        in_specs=[VS] * 4, out_specs=(HS,) * 3 + (VS,) * 2,
+        scratch_shapes=[vf(8, 8, 128), vf(16, 8, 640), vf(16, 8, 640), vf(96, 640), vm(3, 32, 384), vm(2, 48, 256), vm(16, 768), vf(16, 8, 128),
+                        DMA((3, 2, 4)), DMA((3, 2, 4)), DMA((3, 3, 4)), DMA((3, 3, 4)), DMA((3, 4)), DMA((3, 4)), DMA((16,)), DMA((16,)), DMA((16,)), DMA((16,)), DMA((8,)), DMA((8,)), DMA((6,))],
         compiler_params=pltpu.CompilerParams(collective_id=0, has_side_effects=True, vmem_limit_bytes=60 << 20),
         name="gather_attention_weights",
     )(attn, wi, wo, info)
@@ -420,16 +433,25 @@
     return lax.dynamic_update_slice(t, mem_len.astype(F32)[:, None], (3, sq))
 
 
-def scatter_kernel(GA, blkF, gg, oA, oB, oG, accA, sibA, h2, f2, h1, f1, h0, f0, blk, stage, recv, gdp, gsum, gsq,
-                   ss, rs, sib_s, sib_r, loc_s, as_, ar_, is_, ir_, ds_, dr_):
+def scatter_kernel(GA, sumE, sumF, gg, oA, oB, oC, oG, accA, sibA, h2, f2, h1, f1, h0, f0,
+                   accE, accF, hE1, hF1, fE1, fF1, hE0, hF0, fE0, fF0, blk, stage, recv, gdp, gsum, gsq,
+                   ss, rs, sib_s, sib_r, loc_s, as_, ar_, is_, ir_, ds_, dr_, es, er, ld_s):
     me = where_am_i()
     dp, sq = lax.axis_index("dp"), lax.axis_index("seq")
     bar, count = meet(me, "dp")
+    loads = [pltpu.make_async_copy(a, b, ld_s.at[i]) for i, (a, b) in enumerate(((sumE, accE), (sumF, accF)))]
+    for c in loads:
+        c.start()
     pl.semaphore_wait(bar, count)
     hop, fin = staged("A", (h2, f2, h1, f1, h0, f0))
     ring = Scatter(me, PARTS_A, {"A": accA}, hop, fin, ss, rs, {"A": sibA},
                    lambda n, at, c: GA.at[at["x"], at["y"], at["z"], c, n], sib_s, sib_r, loc_s)
+    fhop, ffin = staged("EF", (hE1, hF1, fE1, fF1, hE0, hF0, fE0, fF0))
+    ring_f = Scatter(me, PARTS_G, {"E": accE, "F": accF}, fhop, ffin, es, er)
     ring.start()
+    for c in loads:
+        c.wait()
+    ring_f.hop(1)
 
     def dpx(i):
         peer = (dp + i) % 8
@@ -442,8 +464,11 @@
     ring.hop(2)
     ring.merge(1)
     ring.merge(2)
+    ring_f.pass_on(1)
     ring.pass_on(2)
     ring.merge(3)
+    ring_f.close(1)
+    ring_f.hop(0)
     for i in range(1, 8):
         dpx(i).wait_recv()
     gsum[...] = jnp.sum(gdp[...], axis=0)
@@ -455,10 +480,13 @@
     for i in range(1, 16):
         inf(i).start()
     gsq[sq] = gsum[...]
-    blk[:, 384:640] = blkF[...]
     stage[:, 6:8, :] = jnp.zeros((16, 2, 640), F32)
+    ring_f.pass_on(0)
     ring.close(2)
     ring.hop(1)
+    for n in range(2):
+        blk[48 * n:48 * n + 48, 384:640] = ring_f.result(n)
+    oC[...] = ring_f.result(2)
     ring.pass_on(1)
     ring.close(1)
     ring.hop(0)
@@ -489,20 +517,22 @@
         a2a(i).wait_send()
         inf(i).wait_send()
     ring.drain()
-
-
-def scatter(GA, blkF, gg):
+    ring_f.drain()
+
+
+def scatter(GA, sumE, sumF, gg):
     return pl.pallas_call(
         scatter_kernel,
-        out_shape=(SDS((6, 8, 768), F32), SDS((6, 2, 2048), F32), SDS((8, 128), F32)),
-        in_specs=[HS, VS, VS], out_specs=(VS,) * 3,
-        scratch_shapes=[vm(3, 4, 4, 4, 32, 384), vm(3, 4, 4, 4, 32, 384), *stage_buffers(((3,), (32, 384))),
+        out_shape=(SDS((6, 8, 768), F32), SDS((6, 2, 2048), F32), SDS((16, 768), F32), SDS((8, 128), F32)),
+        in_specs=[HS, HS, HS, VS], out_specs=(VS,) * 4,
+        scratch_shapes=[vm(3, 4, 4, 4, 32, 384), vm(3, 4, 4, 4, 32, 384), *stage_buffers(LEADS, ((3,), (32, 384))),
+                        vm(2, 4, 4, 48, 256), vm(4, 4, 16, 768), *stage_buffers(LEADS[2:], ((2,), (48, 256)), ((), (16, 768))),
                         vf(96, 640), vf(16, 8, 640), vf(16, 8, 640), vf(8, 8, 128), vf(8, 128), vf(16, 8, 128),
                         DMA((3, 3, 4)), DMA((3, 3, 4)), DMA((3, 4)), DMA((3, 4)), DMA((3, 4)),
-                        DMA((16,)), DMA((16,)), DMA((16,)), DMA((16,)), DMA((8,)), DMA((8,))],
+                        DMA((16,)), DMA((16,)), DMA((16,)), DMA((16,)), DMA((8,)), DMA((8,)), DMA((3, 2, 4)), DMA((3, 2, 4)), DMA((2,))],
         compiler_params=pltpu.CompilerParams(collective_id=1, has_side_effects=True, vmem_limit_bytes=60 << 20),
         name="scatter_attention_grads",
-    )(GA, blkF, gg)
+    )(GA, sumE, sumF, gg)
 
 
 def head_masks(value=1.0):
@@ -517,14 +547,6 @@
 def key_positions():
     sq = lax.axis_index("seq")
     return (192 * sq + lax.broadcasted_iota(jnp.int32, (192, 128), 0)).astype(F32)
-
-
-def ffn_place(B, C):
-    def place(n, at):
-        if n < 2:
-            return B.at[at["x"], at["y"], at["z"], at["c"], n]
-        return C.at[at["z"], at["c"], at["x"], at["y"]]
-    return place
 
 
 class Merge:
@@ -595,9 +617,9 @@
     return jnp.concatenate([ref[2 * g, at["x"], at["y"]], ref[2 * g + 1, at["x"], at["y"]]], axis=1)
 
 
-def cross_fwd_kernel(q, lens, blkB, blkC, mem_h, A, q_h, k_h, v_h, kt_h, B, C, o_ref, L_ref,
+def cross_fwd_kernel(q, lens, mem_h, A, B_in, C_in, q_h, k_h, v_h, kt_h, B, C, o_ref, L_ref,
                      qall, mem, wk, wv, wkT, wvT, K, V, KT, VT, ost, mid, one, two, lrow,
-                     mem_s, w_s, out_s, ss, rs, os_, or_, fs, fr, fsib_s, fsib_r, own_s):
+                     mem_s, w_s, out_s, ss, rs, os_, or_, fs, fr, fsib_s, fsib_r):
     me = where_am_i()
     bar, count = meet(me, "z")
 
@@ -614,16 +636,11 @@
 
     for n in range(6):
         qall[n, me["x"], me["y"]] = q[:, 128 * n:128 * n + 128]
-    place = ffn_place(B, C)
-    mine = lambda n: blkB.at[n] if n < 2 else blkC
-    owns = [pltpu.make_async_copy(mine(n), place(n, me), own_s.at[n]) for n in range(3)]
-    for c in owns:
-        c.start()
     lrow[...] = jnp.zeros((4, 2, 8, 128), F32)
     pl.semaphore_wait(bar, count)
     view = lambda n, at: qall.at[n, at["x"], at["y"]]
     plane = Gather(me, PLANE, view, lambda n: view(n, me), ss, rs)
-    ring = Gather(me, [p[2] for p in PARTS_F], place, mine, fs, fr, fsib_s, fsib_r)
+    ring = Gather(me, ("z",) * 3, ffn_place(B, C), None, fs, fr, fsib_s, fsib_r, "xy")
     fold = Merge(me, ost, mid, one, two, os_, or_)
     plane.send(0)
     ring.send(0)
@@ -632,9 +649,6 @@
     for i in range(6):
         wvT[:, 128 * i:128 * i + 128] = wv[128 * i:128 * i + 128, :].T
     plane.forward(0)
-    ring.forward(0)
-    for c in owns:
-        c.wait()
 
     def project(a, b):
         @pl.loop(a // 2, b // 2)
@@ -656,14 +670,11 @@
     project(0, 4)
     plane.send(1, (2, 3))
     plane.send(1, (4, 5))
-    ring.send(1)
     project(4, 10)
     plane.forward(1, (0, 1))
     plane.forward(1, (2, 3))
     project(10, 16)
-    ring.forward(1)
     plane.forward(1, (4, 5))
-    ring.send(2)
     masks = head_masks()
     pos = key_positions()
 
@@ -714,8 +725,8 @@
     out_k = pltpu.make_async_copy(K, k_h, out_s.at[1])
     out_q.start()
     out_k.start()
+    ring.forward(0)
     attend(2)
-    ring.forward(2)
     fold.middle((2, 3))
     fold.send(1, (2, 3))
     for i in range(6):
@@ -743,26 +754,26 @@
     ring.drain()
 
 
-def cross_fwd(q, lens, blkB, blkC, memory, A):
+def cross_fwd(q, lens, memory, A, B, C):
     return pl.pallas_call(
         cross_fwd_kernel,
         out_shape=(SDS((6, 4, 4, 128, 128), BF), SDS((16, 192, 768), BF), SDS((16, 192, 768), BF), SDS((16, 768, 192), BF),
                    SDS((4, 4, 4, 2, 2, 48, 256), BF), SDS((4, 2, 4, 4, 16, 768), BF), SDS((128, 768), F32), SDS((16, 128), F32)),
-        in_specs=[VS] * 4 + [HS] * 2, out_specs=(HS,) * 6 + (VS,) * 2,
+        in_specs=[VS] * 2 + [HS] * 4, out_specs=(HS,) * 6 + (VS,) * 2, input_output_aliases={4: 4, 5: 5},
         scratch_shapes=[vm(6, 4, 4, 128, 128), vm(16, 192, 768), vm(768, 768), vm(768, 768), vm(768, 768), vm(768, 768),
                         vm(16, 192, 768), vm(16, 192, 768), vm(16, 768, 192), vm(16, 768, 192),
                         vm(6, 4, 4, 144, 128), vm(6, 4, 144, 128), vm(6, 3, 4, 144, 128), vm(6, 3, 144, 128), vf(4, 2, 8, 128),
                         DMA((16,)), DMA((4,)), DMA((6,)), DMA((6, 2, 4)), DMA((6, 2, 4)), DMA((6, 2, 3)), DMA((6, 2, 3)),
-                        DMA((3, 3, 4)), DMA((3, 3, 4)), DMA((3, 4)), DMA((3, 4)), DMA((3,))],
+                        DMA((3, 1, 4)), DMA((3, 1, 4)), DMA((3, 4)), DMA((3, 4))],
         compiler_params=pltpu.CompilerParams(collective_id=2, has_side_effects=True, vmem_limit_bytes=60 << 20),
         name="cross_forward",
-    )(q, lens, blkB, blkC, memory, A)
-
-
-def cross_bwd_kernel(do, st, lens, q_h, k_h, v_h, kt_h, mem_h, A, GB, GC, G_in, dq_ref, fB, fC, gm_h, dw_h,
+    )(q, lens, memory, A, B, C)
+
+
+def cross_bwd_kernel(do, st, lens, q_h, k_h, v_h, kt_h, mem_h, A, GB, GC, G_in, dq_ref, gm_h, dw_h, sumE, sumF,
                      qall, doall, stall, wk, wv, K, V, KT, mem, memT, dK, dV, gst, wst, dst, dh1, df1, dh0, df0,
-                     accB, accC, sibB, sibC, hB2, hC2, fB2, fC2, hB1, hC1, fB1, fC1, hB0, hC0, fB0, fC0,
-                     q_s, kv_s, mem_s, w_s, gm_s, dw_s, ss, rs, ds_, dr_, fs, fr, fsib_s, fsib_r, floc):
+                     accB, accC, sibB, sibC, hB2, hC2, fB2, fC2,
+                     q_s, kv_s, mem_s, w_s, gm_s, dw_s, ss, rs, ds_, dr_, fs, fr, fsib_s, fsib_r, floc, sum_s):
     me = where_am_i()
     bar, count = meet(me, "z")
 
@@ -782,10 +793,10 @@
         return stall.at[at["x"], at["y"]] if n == 6 else doall.at[n, at["x"], at["y"]]
 
     plane = Gather(me, PLANE + ("xy",), place, lambda n: place(n, me), ss, rs)
-    fhop, ffin = staged("BC", (hB2, hC2, fB2, fC2, hB1, hC1, fB1, fC1, hB0, hC0, fB0, fC0))
+    fhop, ffin = staged("BC", (hB2, hC2, fB2, fC2))
     grads = ffn_place(GB, GC)
     ring = Scatter(me, PARTS_F, {"B": accB, "C": accC}, fhop, ffin, fs, fr, {"B": sibB, "C": sibC},
-                   lambda n, at, c: grads(n, {**at, "c": c}), fsib_s, fsib_r, floc)
+                   lambda n, at, c: grads(n, {**at, "c": c}), fsib_s, fsib_r, floc, "xy")
     back = Scatter(me, PARTS_D, {"D": dst}, {1: {"D": dh1}, 0: {"D": dh0}}, {1: {"D": df1}, 0: {"D": df0}}, ds_, dr_)
     plane.send(0, (6, 0, 1, 2, 3, 4, 5))
     ring.start()
@@ -809,13 +820,13 @@
     plane.send(1, (2, 3))
     plane.send(1, (4, 5))
     ring.merge(0)
-    ring.hop(2)
+    ring.hop(0)
     turn(3, 6)
     plane.forward(1, (6, 0, 1))
     ring.merge(1)
     ring.merge(2)
     plane.forward(1, (2, 3))
-    ring.pass_on(2)
+    ring.pass_on(0)
     masks = head_masks()
     pos = key_positions()
 
@@ -922,8 +933,6 @@
                 dw_copy(k, r, 1).start()
 
     turn(6, 12)
-    ring.close(2)
-    ring.hop(1)
     back.pass_on(1, (4, 5))
     back.close(1, (2, 3))
     back.hop(0, (2, 3))
@@ -932,19 +941,17 @@
     back.close(1, (4, 5))
     back.hop(0, (4, 5))
     back.pass_on(0, (2, 3))
-    ring.pass_on(1)
     mem_grad(4, 8)
+    ring.close(0)
+    sums = [pltpu.make_async_copy(accB.at[:, :, :, me["z"]], sumE, sum_s.at[0]), pltpu.make_async_copy(accC.at[me["z"]], sumF, sum_s.at[1])]
+    for c in sums:
+        c.start()
     back.pass_on(0, (4, 5))
-    ring.close(1)
-    ring.hop(0)
-    weight_grad(0, 1)
-    ring.pass_on(0)
-    weight_grad(1, 3)
+    weight_grad(0, 3)
     for n in range(6):
         dq_ref[:, 128 * n:128 * n + 128] = (0.125 * back.result(n)).T
-    fB[0:48, :] = ring.result(0)
-    fB[48:96, :] = ring.result(1)
-    fC[...] = ring.result(2)
+    for c in sums:
+        c.wait()
     gm_copy(6).wait()
     gm_copy(7).wait()
     for k in range(2):
@@ -959,14 +966,14 @@
     bB, bC = (48, 256), (16, 768)
     return pl.pallas_call(
         cross_bwd_kernel,
-        out_shape=(SDS((128, 768), F32), SDS((96, 256), F32), SDS((16, 768), F32), SDS((8, 384, 768), F32), SDS((16, 768, 384), BF)),
-        in_specs=[VS] * 3 + [HS] * 9, out_specs=(VS,) * 3 + (HS,) * 2, input_output_aliases={11: 4},
+        out_shape=(SDS((128, 768), F32), SDS((8, 384, 768), F32), SDS((16, 768, 384), BF), SDS((2, 4, 4, 48, 256), BF), SDS((4, 4, 16, 768), BF)),
+        in_specs=[VS] * 3 + [HS] * 9, out_specs=(VS,) + (HS,) * 4, input_output_aliases={11: 2},
         scratch_shapes=[vm(6, 4, 4, 128, 128), vm(6, 4, 4, 128, 128), vf(4, 4, 24, 128), vm(768, 768), vm(768, 768),
                         vm(2, 4, 192, 256), vm(2, 4, 192, 256), vm(2, 4, 256, 192), vm(4, 256, 768), vm(768, 3072), vm(3072, 768), vm(3072, 768),
                         vf(2, 384, 768), vm(2, 256, 768), vm(6, 4, 4, 128, 128), vm(6, 2, 2, 128, 128), vm(6, 2, 4, 128, 128), vm(6, 2, 128, 128), vm(6, 2, 128, 128),
-                        vm(2, 4, 4, 4, *bB), vm(4, 4, 4, *bC), vm(2, 4, 4, 4, *bB), vm(4, 4, 4, *bC), *stage_buffers(((2,), bB), ((), bC)),
+                        vm(2, 4, 4, 4, *bB), vm(4, 4, 4, *bC), vm(2, 4, 4, 4, *bB), vm(4, 4, 4, *bC), *stage_buffers(LEADS[:2], ((2,), bB), ((), bC)),
                         DMA, DMA((3, 2, 4)), DMA((4,)), DMA((4,)), DMA((2,)), DMA((2, 2)), DMA((7, 2, 4)), DMA((7, 2, 4)), DMA((6, 2, 4)), DMA((6, 2, 4)),
-                        DMA((3, 3, 4)), DMA((3, 3, 4)), DMA((3, 4)), DMA((3, 4)), DMA((3, 4))],
+                        DMA((3, 1, 4)), DMA((3, 1, 4)), DMA((3, 4)), DMA((3, 4)), DMA((3, 4)), DMA((2,))],
         compiler_params=pltpu.CompilerParams(collective_id=3, has_side_effects=True, vmem_limit_bytes=60 << 20),
         name="cross_backward",
     )(do, st, lens, q_h, k_h, v_h, kt_h, memory.reshape(3072, 768), A, GB, GC, GA)
@@ -1080,30 +1087,37 @@
     dh = jnp.zeros((128, 768), F32)
     c0 = 0.7978845608028654
     sB, sC = [], []
-    for j in range(8):
-        lB[j].wait()
-        lB[8 + j].wait()
-        lC[j].wait()
-        a = dot(h, WB[j])
-        up = dot(h, WB[8 + j])
-        t = jnp.tanh(c0 * (a + 0.044715 * a * a * a))
-        half = 0.5 * (1.0 + t)
-        gel = a * half
-        der = half + 0.5 * a * (1.0 - t * t) * (c0 * (1.0 + 0.134145 * a * a))
-        mid32 = gel * up
-        mid = mid32.astype(BF)
-        y += dot(mid, WC[j])
-        dm = dot(df, WC[j], 1, 1)
-        dga = (dm * up * der).astype(BF)
-        dup = (dm * gel).astype(BF)
-        dh += dot(dga, WB[j], 1, 1) + dot(dup, WB[8 + j], 1, 1)
-        gB[j] = dot(hT, dga).astype(BF)
-        gB[8 + j] = dot(hT, dup).astype(BF)
-        gC[j] = dot(flip(mid32).astype(BF), df).astype(BF)
-        sB += [pltpu.make_async_copy(gB.at[j], GB.at[j], tb.at[j]), pltpu.make_async_copy(gB.at[8 + j], GB.at[8 + j], tb.at[8 + j])]
-        sC += [pltpu.make_async_copy(gC.at[j], GC.at[j], tc.at[j])]
-        for c in sB[-2:] + sC[-1:]:
-            c.start()
+    for j0 in range(0, 8, 2):
+        js = range(j0, j0 + 2)
+        for j in js:
+            lB[j].wait()
+            lB[8 + j].wait()
+            lC[j].wait()
+        a_s = [dot(h, WB[j]) for j in js]
+        ups = [dot(h, WB[8 + j]) for j in js]
+        dms = [dot(df, WC[j], 1, 1) for j in js]
+        mids, dgs, dus = [], [], []
+        for a, up, dm in zip(a_s, ups, dms):
+            t = jnp.tanh(c0 * (a + 0.044715 * a * a * a))
+            half = 0.5 * (1.0 + t)
+            gel = a * half
+            der = half + 0.5 * a * (1.0 - t * t) * (c0 * (1.0 + 0.134145 * a * a))
+            mids.append(gel * up)
+            dgs.append((dm * up * der).astype(BF))
+            dus.append((dm * gel).astype(BF))
+        y += dot(jnp.concatenate([m.astype(BF) for m in mids], axis=1), WC[j0:j0 + 2].reshape(2 * 256, 768))
+        for n, j in enumerate(js):
+            dh += dot(dgs[n], WB[j], 1, 1) + dot(dus[n], WB[8 + j], 1, 1)
+        for n, j in enumerate(js):
+            gB[j] = dot(hT, dgs[n]).astype(BF)
+            gB[8 + j] = dot(hT, dus[n]).astype(BF)
+            gC[j] = dot(flip(mids[n]).astype(BF), df).astype(BF)
+        for j in js:
+            new = [pltpu.make_async_copy(gB.at[j], GB.at[j], tb.at[j]), pltpu.make_async_copy(gB.at[8 + j], GB.at[8 + j], tb.at[8 + j]),
+                   pltpu.make_async_copy(gC.at[j], GC.at[j], tc.at[j])]
+            for c in new:
+                c.start()
+            sB += new
     out[...] = (x + y).astype(BF)
     dz, gain = rms_back(x, inv, gains[2:3, :], dh)
     gg[...] = gain
@@ -1274,18 +1288,18 @@
 ):
     swap = lambda a: a.transpose(1, 0, 2)
     attn_t, in_t = swap(attn_master), swap(ffn_in_master)
-    gath_a, gains, lens, blk_b, blk_c = gather(attn_t, in_t, ffn_out_master, info_tile(gain_master, mem_len))
+    gath_a, gath_b, gath_c, gains, lens = gather(attn_t, in_t, ffn_out_master, info_tile(gain_master, mem_len))
     aw = gath_a.reshape(16, 768, 384)
     x = dec_input[0]
     q2, h1, qkv, o1, x1, h2, L1 = self_fwd(x, gains, aw)
-    q_all, k_two, v_two, kt_two, gath_b, gath_c, o2, L2 = cross_fwd(q2, lens, blk_b, blk_c, memory, aw)
+    q_all, k_two, v_two, kt_two, gath_b, gath_c, o2, L2 = cross_fwd(q2, lens, memory, aw, gath_b, gath_c)
     out_block, do2, st, dx2, g3, GA, GB, GC = ffn(x1, o2, L2, grad_out[0], gains, aw, gath_b.reshape(16, 768, 256), gath_c.reshape(8, 256, 768))
-    dq2, blk_f, share_c, gm, GA = cross_bwd(
+    dq2, gm, GA, sum_b, sum_c = cross_bwd(
         do2, st, lens, q_all, k_two, v_two, kt_two, memory, aw,
         GB.reshape(4, 4, 4, 2, 2, 48, 256), GC.reshape(4, 2, 4, 4, 16, 768), GA,
     )
     grad_input, tile_g, GA, grad_memory = self_bwd(dq2, h2, x1, dx2, qkv, o1, L1, x, h1, gains, g3, aw, GA, gm.reshape(16, 192, 768))
-    share_a, share_b, share_g = scatter(GA.reshape(4, 4, 4, 2, 3, 32, 384), blk_f, tile_g)
+    share_a, share_b, share_c, share_g = scatter(GA.reshape(4, 4, 4, 2, 3, 32, 384), sum_b, sum_c, tile_g)
     new = adam(
         attn_t, swap(attn_first), swap(attn_second), share_a,
         in_t, swap(ffn_in_first), swap(ffn_in_second), share_b,

time: 318 us -> 296 us (0.931)
  Pallas kernels: 310 us -> 288 us
    pallas_call x1, Pallas kernels: 80.9 us -> 62 us  [cross_fwd(): pl.pallas_call(cross_fwd_kernel, out_shape=(SDS((6, 4, 4, 128, 128), BF),...]
    pallas_call x1, Pallas kernels: 86.3 us -> 82.5 us  [cross_bwd(): pl.pallas_call(cross_bwd_kernel, out_shape=(SDS((128, 768), F32), SDS((8,...]
where the time goes in v1:
time: 296 us; the launch traced here: 291 us
  Pallas kernels  288 us (97%)
    pallas_call x1, Pallas kernels, cross_bwd(): pl.pallas_call(cross_bwd_kernel, out_shape=(SDS((128, 768), F32), SDS((8,...  82.5 us
    pallas_call x1, Pallas kernels, cross_fwd(): pl.pallas_call(cross_fwd_kernel, out_shape=(SDS((6, 4, 4, 128, 128), BF),...  62 us
    pallas_call x1, Pallas kernels, gather(): pl.pallas_call(gather_kernel, out_shape=(SDS((4, 4, 4, 2, 3, 32, 384), BF...  52.9 us
    pallas_call x1, Pallas kernels, scatter(): pl.pallas_call(scatter_kernel, out_shape=(SDS((6, 8, 768), F32), SDS((6,...  51.8 us
    pallas_call x1, Pallas kernels, ffn(): pl.pallas_call(ffn_kernel, out_shape=(SDS((128, 768), BF), SDS((128, 768)...  16.3 us
    pallas_call x1, Pallas kernels, self_bwd(): pl.pallas_call(self_bwd_kernel, out_shape=(SDS((128, 768), F32), SDS((8,...  13.7 us

profile of v1, /device:TPU:0, one launch (start us, length us, event | category | flops | bytes accessed | tf_op | source)
XLA Modules:
  0.0 290.8 jit_solution(7526518885339831372)
XLA Ops:
  1.3 0.7 convert_convert_fusion
  2.0 0.2 dynamic_update_slice.6
  2.2 0.1 dynamic_update_slice.7.info
  2.3 0.0 copy-start
  2.3 0.6 copy-done
  2.9 52.9 %gather_attention_weights.1 = (bf16[4,4,4,2,3,32,384]{6,5,4,3,2,1,0:T(8,128)(2,1)}, bf16[4,4,4,2,2,48,256]{6,5,4,3,2,1,0:T(8,128)(2,1)}, bf16[4,2,4,4,16,768]{5,...) custom-call(f32[6,8,768]{2,1,0:T(8,128)} %bitcast.41, f32[6,2,2048]{2,1,0:T(2,128)} %bitcast.43, f32[16,768]{1,0:T(8,128)} %refs_8_.1, ...), custom_call_target="tpu_custom_call" | custom-call | tf_op jit(solution)/shard_map/gather_attention_weights/pallas_call | solution.py:418
  55.8 5.9 %self_forward.1 = (bf16[128,768]{1,0:T(8,128)(2,1)}, bf16[128,768]{1,0:T(8,128)(2,1)}, bf16[3,128,768]{2,1,0:T(8,128)(2,1)}, bf16[128,768]{1,0:T(8,128)(2,1)}, f...) custom-call(bf16[128,768]{1,0:T(8,128)(2,1)} %bitcast.39, f32[8,768]{1,0:T(8,128)} %get-tuple-element.76.gains, ...), custom_call_target="tpu_custom_call" | custom-call | tf_op jit(solution)/shard_map/self_forward/pallas_call | solution.py:1057
  61.7 62.0 %cross_forward.1 = (bf16[6,4,4,128,128]{4,3,2,1,0:T(8,128)(2,1)}, bf16[16,192,768]{2,1,0:T(8,128)(2,1)}, bf16[16,192,768]{2,1,0:T(8,128)(2,1)}, bf16[16,768,192]...) custom-call(bf16[128,768]{1,0:T(8,128)(2,1)} %get-tuple-element.79.q, ...), custom_call_target="tpu_custom_call", output_to_operand_aliasing={{4}: (4, {}), {5}: (5, {})} | custom-call | tf_op jit(solution)/shard_map/cross_forward/pallas_call | solution.py:758
  123.7 16.3 %feed_forward.1 = (bf16[128,768]{1,0:T(8,128)(2,1)}, bf16[128,768]{1,0:T(8,128)(2,1)}, f32[24,128]{1,0:T(8,128)}, f32[128,768]{1,0:T(8,128)}, f32[1,768]{1,0:T(1...) custom-call(f32[128,768]{1,0:T(8,128)} %get-tuple-element.78.x1, ...), custom_call_target="tpu_custom_call" | custom-call | tf_op jit(solution)/shard_map/feed_forward/pallas_call | solution.py:1145
  140.0 82.5 %cross_backward.1 = (f32[128,768]{1,0:T(8,128)}, f32[8,384,768]{2,1,0:T(8,128)}, bf16[16,768,384]{2,1,0:T(8,128)(2,1)}, bf16[2,4,4,48,256]{4,3,2,1,0:T(8,128)(2,1)}, bf16[4,4,16,768]{3,2,1,0:T(8,128)(2,1)}) custom-call(bf16[128,768]{1,0:T(8,128)(2,1)} %get-tuple-element.88.do, f32[24,128]{1,0:T(8,128)} %get-tuple-element.89.st, ...), custom_call_target="tpu_custom_call", output_to_operand_aliasing={{2}: (11, {})} | custom-call | tf_op jit(solution)/shard_map/cross_backward/pallas_call | solution.py:967
  222.6 13.7 %self_backward.1 = (f32[128,768]{1,0:T(8,128)}, f32[8,8,128]{2,1,0:T(8,128)}, bf16[16,768,384]{2,1,0:T(8,128)(2,1)}, f32[16,192,768]{2,1,0:T(8,128)}) custom-call(f32[128,768]{1,0:T(8,128)} %get-tuple-element.97.dq2, bf16[128,768]{1,0:T(8,128)(2,1)} %get-tuple-element.98.h2, f32[128,768]{1,0:T(8,128)} %get-tuple-element.78.x1, ...), custom_call_target="tpu_custom_call", output_to_operand_aliasing={{2}: (12, {})} | custom-call | tf_op jit(solution)/shard_map/self_backward/pallas_call | solution.py:1244
  236.3 51.8 %scatter_attention_grads.1 = (f32[6,8,768]{2,1,0:T(8,128)}, f32[6,2,2048]{2,1,0:T(2,128)}, f32[16,768]{1,0:T(8,128)}, f32[8,128]{1,0:T(8,128)}) custom-call(bf16[4,4,4,2,3,32,384]{6,5,4,3,2,1,0:T(8,128)(2,1)} %bitcast.32, bf16[2,4,4,48,256]{4,3,2,1,0:T(8,128)(2,1)} %get-tuple-element.110.sumE, bf16[4,4,16,768]{3,2,1,0:T(8,128)(2,1)} %get-tuple-element.111.sumF, ...), custom_call_target="tpu_custom_call" | custom-call | tf_op jit(solution)/shard_map/scatter_attention_grads/pallas_call | solution.py:524
  288.1 2.5 adam.1
  (1 shorter events, 0.0 us)
Async XLA Ops:
  2.3 0.6 copy-start

commit v2 on v1

--- a/solution.py
+++ b/solution.py
@@ -96,18 +96,18 @@
             at[axes[0]] = pl.ds(2 * half, 2)
         return at
 
-    def kinds(self, n, t):
-        return (0, 1, 2, 3) if t or self.whole else (0, 1, 2 + n % 2)
+    def kinds(self, t):
+        return (0, 1, 2, 3) if t == self.last else (0, 1, 2)
 
     def copy(self, n, t, kind, back=0):
-        axis = self.orders[n][t]
-        step = 1 if kind in (0, 2) else -1
-        dst = self.view(n, self.group(n, t, back) if kind < 2 else self.group(n, t, back - step, kind - 2))
-        src = self.own(n) if self.own and t == 0 and kind < 2 and back == 0 else dst
-        return remote(src, dst, self.ss.at[n, t, kind], self.rs.at[n, t, kind], moved(self.me, axis, step))
+        straight = kind < 2 or t < self.last
+        step = (1, -1, 2 if straight else 1, -1)[kind]
+        dst = self.view(n, self.group(n, t, back) if straight else self.group(n, t, back - step, kind - 2))
+        src = self.own(n) if self.own and t == 0 and straight and back == 0 else dst
+        return remote(src, dst, self.ss.at[n, t, kind], self.rs.at[n, t, kind], moved(self.me, self.orders[n][t], step))
 
     def arrived(self, n, t, kind):
-        self.copy(n, t, kind, -1 if kind in (0, 2) else 1).wait_recv()
+        self.copy(n, t, kind, (-1, 1, -2 if t < self.last else -1, 1)[kind]).wait_recv()
 
     def sibling(self, n, j, c):
         v = self.view(n, {**self.group(n, self.last, (0, -1, 1, 2)[j]), "c": c})
@@ -116,20 +116,19 @@
     def send(self, t, ns=None):
         for n in ns or range(self.count):
             if t:
-                for k in self.kinds(n, t - 1)[2:]:
+                for k in range(3):
                     self.arrived(n, t - 1, k)
-            self.copy(n, t, 0).start()
-            self.copy(n, t, 1).start()
+            for k in (0, 1) if t == self.last else (2, 0, 1):
+                self.copy(n, t, k).start()
             if self.sib_s is not None and t == self.last:
                 self.sibling(n, 0, self.me["c"]).start()
 
-    def forward(self, t, ns=None):
+    def forward(self, ns=None):
         for n in ns or range(self.count):
             for k in (0, 1):
-                self.arrived(n, t, k)
-                if 2 + k in self.kinds(n, t):
-                    self.copy(n, t, 2 + k).start()
-                if self.sib_s is not None and t == self.last:
+                self.arrived(n, self.last, k)
+                self.copy(n, self.last, 2 + k).start()
+                if self.sib_s is not None:
                     self.sibling(n, 1 + k, self.me["c"]).start()
 
     def finish(self, ns=None):
@@ -147,7 +146,7 @@
     def drain(self):
         for n in range(self.count):
             for t in range(self.last + 1):
-                for k in self.kinds(n, t):
+                for k in self.kinds(t):
                     self.copy(n, t, k).wait_send()
             if self.sib_s is not None:
                 for j in range(4):
@@ -182,21 +181,21 @@
             at[axes[0]] = pl.ds(2 * half, 2)
         return at
 
-    def kinds(self, n, t):
-        return (0, 1) if t or self.whole else (n % 2,)
+    def fins(self, t):
+        return 2 if t == self.last else 3
 
     def refs(self, n, t):
         name = self.parts[n][0]
-        return self.acc[name], self.hop_b[t][name], self.fin_b[t][name]
-
-    def hop_copy(self, n, t, kind):
-        step = 1 if kind == 0 else -1
+        return self.acc[name], self.hop_b[name] if t == self.last else None, self.fin_b[t][name]
+
+    def hop_copy(self, n, kind):
+        step, t = 1 if kind == 0 else -1, self.last
         a, h, _ = self.refs(n, t)
         return remote(a.at[self.idx(n, self.group(n, t, 2 * step, kind))], h.at[self.slot(n) + (kind,)],
                       self.ss.at[n, t, kind], self.rs.at[n, t, kind], moved(self.me, self.parts[n][2][t], step))
 
     def fin_copy(self, n, t, kind):
-        step = 1 if kind == 0 else -1
+        step = (1, -1, 2)[kind]
         a, _, f = self.refs(n, t)
         return remote(a.at[self.idx(n, self.group(n, t, step))], f.at[self.slot(n) + (kind,)],
                       self.ss.at[n, t, 2 + kind], self.rs.at[n, t, 2 + kind], moved(self.me, self.parts[n][2][t], step))
@@ -248,72 +247,78 @@
             a, b = self.acc[self.parts[n][0]], self.sib[self.parts[n][0]]
 
             def fn(i, _):
-                a[i] = (a[i].astype(F32) + b[i].astype(F32)).astype(BF)
+                a[i] = a[i] + b[i]
 
             self.each(n, self.last, self.group(n, self.last, STEPS[j]), fn)
 
-    def hop(self, t, ns=None):
+    def send(self, t, ns=None):
         for n in ns or range(self.count):
-            for k in self.kinds(n, t):
-                self.hop_copy(n, t, k).start()
-
-    def pass_on(self, t, ns=None):
+            if t == self.last:
+                for k in (0, 1):
+                    self.hop_copy(n, k).start()
+            else:
+                for k in (2, 0, 1):
+                    self.fin_copy(n, t, k).start()
+
+    def forward(self, ns=None):
+        t = self.last
         for n in ns or range(self.count):
             a, h, _ = self.refs(n, t)
             for k in (0, 1):
-                if k in self.kinds(n, t):
-                    self.hop_copy(n, t, k).wait_recv()
-
-                    def fn(i, pos):
-                        j = self.slot(n) + (k,) + pos
-                        a[i] = (a[i].astype(F32) + h[j].astype(F32)).astype(BF)
-
-                    self.each(n, t, self.group(n, t, 1 if k == 0 else -1), fn, k)
+                self.hop_copy(n, k).wait_recv()
+
+                def fn(i, pos):
+                    a[i] = a[i] + h[self.slot(n) + (k,) + pos]
+
+                self.each(n, t, self.group(n, t, 1 if k == 0 else -1), fn, k)
                 self.fin_copy(n, t, k).start()
 
     def close(self, t, ns=None):
         for n in ns or range(self.count):
-            self.fin_copy(n, t, 0).wait_recv()
-            self.fin_copy(n, t, 1).wait_recv()
+            for k in range(self.fins(t)):
+                self.fin_copy(n, t, k).wait_recv()
             a, _, f = self.refs(n, t)
 
             def fn(i, pos):
-                s = self.slot(n)
-                a[i] = (a[i].astype(F32) + f[s + (0,) + pos].astype(F32) + f[s + (1,) + pos].astype(F32)).astype(BF)
+                v = a[i].astype(F32)
+                for k in range(self.fins(t)):
+                    v = v + f[self.slot(n) + (k,) + pos].astype(F32)
+                a[i] = v.astype(BF)
 
             self.each(n, t, self.group(n, t, 0), fn)
 
     def result(self, n):
-        self.fin_copy(n, 0, 0).wait_recv()
-        self.fin_copy(n, 0, 1).wait_recv()
         a, _, f = self.refs(n, 0)
-        s = self.slot(n)
-        return a[self.idx(n, self.me)].astype(F32) + f[s + (0,)].astype(F32) + f[s + (1,)].astype(F32)
+        v = a[self.idx(n, self.me)].astype(F32)
+        for k in range(3):
+            self.fin_copy(n, 0, k).wait_recv()
+            v = v + f[self.slot(n) + (k,)].astype(F32)
+        return v
 
     def drain(self):
         for n in range(self.count):
             if self.sib is not None:
                 for j in range(4):
                     self.sib_copy(n, j).wait_send()
+            for k in (0, 1):
+                self.hop_copy(n, k).wait_send()
             for t in range(self.last + 1):
-                for k in self.kinds(n, t):
-                    self.hop_copy(n, t, k).wait_send()
-                self.fin_copy(n, t, 0).wait_send()
-                self.fin_copy(n, t, 1).wait_send()
+                for k in range(self.fins(t)):
+                    self.fin_copy(n, t, k).wait_send()
+
+
+LEAD_A = ((2, 2, 4), (2, 4, 4), (3, 4), (3,))
+LEAD_D = ((2, 2), (2, 4), (3,))
 
 
 def stage_buffers(leads, *shapes):
     return [vm(*pre, *lead, *block) for lead in leads for pre, block in shapes]
-
-
-LEADS = ((2, 2, 4), (2, 4, 4), (2, 2), (2, 4), (2,), (2,))
 
 
 def staged(names, refs):
     k = len(names)
     got = [dict(zip(names, refs[k * i:k * i + k])) for i in range(len(refs) // k)]
-    last = len(got) // 2 - 1
-    return {last - t: got[2 * t] for t in range(last + 1)}, {last - t: got[2 * t + 1] for t in range(last + 1)}
+    return got[0], {len(got) - 2 - i: g for i, g in enumerate(got[1:])}
 
 
 def ffn_place(B, C):
@@ -369,15 +374,12 @@
         o.start()
     ring.send(0)
     ring_f.send(0)
-    ring.forward(0)
-    ring_f.forward(0)
     for o in owns:
         o.wait()
     ring.send(1)
     ring_f.send(1)
-    ring.forward(1)
     ring.send(2)
-    ring_f.forward(1)
+    ring_f.forward()
     for i in range(1, 16):
         inf(i).wait_recv()
     tile = jnp.sum(irecv[...], axis=0)
@@ -389,7 +391,7 @@
 
     for i in range(1, 8):
         dpx(i).start()
-    ring.forward(2)
+    ring.forward()
     for i in range(1, 8):
         dpx(i, i).wait_recv()
     lane = lax.broadcasted_iota(jnp.int32, (8, 128), 1)
@@ -433,8 +435,8 @@
     return lax.dynamic_update_slice(t, mem_len.astype(F32)[:, None], (3, sq))
 
 
-def scatter_kernel(GA, sumE, sumF, gg, oA, oB, oC, oG, accA, sibA, h2, f2, h1, f1, h0, f0,
-                   accE, accF, hE1, hF1, fE1, fF1, hE0, hF0, fE0, fF0, blk, stage, recv, gdp, gsum, gsq,
+def scatter_kernel(GA, sumE, sumF, gg, oA, oB, oC, oG, accA, sibA, h2, f2, f1, f0,
+                   accE, accF, hE1, hF1, fE1, fF1, fE0, fF0, blk, stage, recv, gdp, gsum, gsq,
                    ss, rs, sib_s, sib_r, loc_s, as_, ar_, is_, ir_, ds_, dr_, es, er, ld_s):
     me = where_am_i()
     dp, sq = lax.axis_index("dp"), lax.axis_index("seq")
@@ -443,15 +445,15 @@
     for c in loads:
         c.start()
     pl.semaphore_wait(bar, count)
-    hop, fin = staged("A", (h2, f2, h1, f1, h0, f0))
+    hop, fin = staged("A", (h2, f2, f1, f0))
     ring = Scatter(me, PARTS_A, {"A": accA}, hop, fin, ss, rs, {"A": sibA},
                    lambda n, at, c: GA.at[at["x"], at["y"], at["z"], c, n], sib_s, sib_r, loc_s)
-    fhop, ffin = staged("EF", (hE1, hF1, fE1, fF1, hE0, hF0, fE0, fF0))
+    fhop, ffin = staged("EF", (hE1, hF1, fE1, fF1, fE0, fF0))
     ring_f = Scatter(me, PARTS_G, {"E": accE, "F": accF}, fhop, ffin, es, er)
     ring.start()
     for c in loads:
         c.wait()
-    ring_f.hop(1)
+    ring_f.send(1)
 
     def dpx(i):
         peer = (dp + i) % 8
@@ -461,14 +463,14 @@
         dpx(i).start()
     gdp[dp] = gg[dp]
     ring.merge(0)
-    ring.hop(2)
+    ring.send(2)
     ring.merge(1)
     ring.merge(2)
-    ring_f.pass_on(1)
-    ring.pass_on(2)
+    ring_f.forward()
+    ring.forward()
     ring.merge(3)
     ring_f.close(1)
-    ring_f.hop(0)
+    ring_f.send(0)
     for i in range(1, 8):
         dpx(i).wait_recv()
     gsum[...] = jnp.sum(gdp[...], axis=0)
@@ -481,16 +483,13 @@
         inf(i).start()
     gsq[sq] = gsum[...]
     stage[:, 6:8, :] = jnp.zeros((16, 2, 640), F32)
-    ring_f.pass_on(0)
     ring.close(2)
-    ring.hop(1)
+    ring.send(1)
     for n in range(2):
         blk[48 * n:48 * n + 48, 384:640] = ring_f.result(n)
     oC[...] = ring_f.result(2)
-    ring.pass_on(1)
     ring.close(1)
-    ring.hop(0)
-    ring.pass_on(0)
+    ring.send(0)
     for n in range(3):
         blk[32 * n:32 * n + 32, 0:384] = ring.result(n)
     for k in range(16):
@@ -525,11 +524,11 @@
         scatter_kernel,
         out_shape=(SDS((6, 8, 768), F32), SDS((6, 2, 2048), F32), SDS((16, 768), F32), SDS((8, 128), F32)),
         in_specs=[HS, HS, HS, VS], out_specs=(VS,) * 4,
-        scratch_shapes=[vm(3, 4, 4, 4, 32, 384), vm(3, 4, 4, 4, 32, 384), *stage_buffers(LEADS, ((3,), (32, 384))),
-                        vm(2, 4, 4, 48, 256), vm(4, 4, 16, 768), *stage_buffers(LEADS[2:], ((2,), (48, 256)), ((), (16, 768))),
+        scratch_shapes=[vm(3, 4, 4, 4, 32, 384), vm(3, 4, 4, 4, 32, 384), *stage_buffers(LEAD_A, ((3,), (32, 384))),
+                        vm(2, 4, 4, 48, 256), vm(4, 4, 16, 768), *stage_buffers(LEAD_D, ((2,), (48, 256)), ((), (16, 768))),
                         vf(96, 640), vf(16, 8, 640), vf(16, 8, 640), vf(8, 8, 128), vf(8, 128), vf(16, 8, 128),
-                        DMA((3, 3, 4)), DMA((3, 3, 4)), DMA((3, 4)), DMA((3, 4)), DMA((3, 4)),
-                        DMA((16,)), DMA((16,)), DMA((16,)), DMA((16,)), DMA((8,)), DMA((8,)), DMA((3, 2, 4)), DMA((3, 2, 4)), DMA((2,))],
+                        DMA((3, 3, 5)), DMA((3, 3, 5)), DMA((3, 4)), DMA((3, 4)), DMA((3, 4)),
+                        DMA((16,)), DMA((16,)), DMA((16,)), DMA((16,)), DMA((8,)), DMA((8,)), DMA((3, 2, 5)), DMA((3, 2, 5)), DMA((2,))],
         compiler_params=pltpu.CompilerParams(collective_id=1, has_side_effects=True, vmem_limit_bytes=60 << 20),
         name="scatter_attention_grads",
     )(GA, sumE, sumF, gg)
@@ -648,7 +647,6 @@
         c.wait()
     for i in range(6):
         wvT[:, 128 * i:128 * i + 128] = wv[128 * i:128 * i + 128, :].T
-    plane.forward(0)
 
     def project(a, b):
         @pl.loop(a // 2, b // 2)
@@ -671,10 +669,10 @@
     plane.send(1, (2, 3))
     plane.send(1, (4, 5))
     project(4, 10)
-    plane.forward(1, (0, 1))
-    plane.forward(1, (2, 3))
+    plane.forward((0, 1))
+    plane.forward((2, 3))
     project(10, 16)
-    plane.forward(1, (4, 5))
+    plane.forward((4, 5))
     masks = head_masks()
     pos = key_positions()
 
@@ -725,7 +723,7 @@
     out_k = pltpu.make_async_copy(K, k_h, out_s.at[1])
     out_q.start()
     out_k.start()
-    ring.forward(0)
+    ring.forward()
     attend(2)
     fold.middle((2, 3))
     fold.send(1, (2, 3))
@@ -771,7 +769,7 @@
 
 
 def cross_bwd_kernel(do, st, lens, q_h, k_h, v_h, kt_h, mem_h, A, GB, GC, G_in, dq_ref, gm_h, dw_h, sumE, sumF,
-                     qall, doall, stall, wk, wv, K, V, KT, mem, memT, dK, dV, gst, wst, dst, dh1, df1, dh0, df0,
+                     qall, doall, stall, wk, wv, K, V, KT, mem, memT, dK, dV, gst, wst, dst, dh1, df1, df0,
                      accB, accC, sibB, sibC, hB2, hC2, fB2, fC2,
                      q_s, kv_s, mem_s, w_s, gm_s, dw_s, ss, rs, ds_, dr_, fs, fr, fsib_s, fsib_r, floc, sum_s):
     me = where_am_i()
@@ -797,7 +795,7 @@
     grads = ffn_place(GB, GC)
     ring = Scatter(me, PARTS_F, {"B": accB, "C": accC}, fhop, ffin, fs, fr, {"B": sibB, "C": sibC},
                    lambda n, at, c: grads(n, {**at, "c": c}), fsib_s, fsib_r, floc, "xy")
-    back = Scatter(me, PARTS_D, {"D": dst}, {1: {"D": dh1}, 0: {"D": dh0}}, {1: {"D": df1}, 0: {"D": df0}}, ds_, dr_)
+    back = Scatter(me, PARTS_D, {"D": dst}, *staged("D", (dh1, df1, df0)), ds_, dr_)
     plane.send(0, (6, 0, 1, 2, 3, 4, 5))
     ring.start()
     for c in loads:
@@ -813,20 +811,18 @@
             def _():
                 load_mem(e + 4).start()
 
-    turn(0, 1)
-    plane.forward(0, (6, 0, 1, 2, 3, 4, 5))
-    turn(1, 3)
+    turn(0, 3)
     plane.send(1, (6, 0, 1))
     plane.send(1, (2, 3))
     plane.send(1, (4, 5))
     ring.merge(0)
-    ring.hop(0)
+    ring.send(0)
     turn(3, 6)
-    plane.forward(1, (6, 0, 1))
+    plane.forward((6, 0, 1))
     ring.merge(1)
     ring.merge(2)
-    plane.forward(1, (2, 3))
-    ring.pass_on(0)
+    plane.forward((2, 3))
+    ring.forward()
     masks = head_masks()
     pos = key_positions()
 
@@ -886,20 +882,20 @@
 
         if g < 2:
             fetch_kv(g + 1, 0)
-        back.hop(1, (2 * g, 2 * g + 1))
+        back.send(1, (2 * g, 2 * g + 1))
 
     plane.finish((6, 0, 1))
     attend(0)
-    plane.forward(1, (4, 5))
+    plane.forward((4, 5))
     plane.finish((2, 3))
     attend(1)
-    back.pass_on(1, (0, 1))
+    back.forward((0, 1))
     ring.merge(3)
     plane.finish((4, 5))
     attend(2)
-    back.pass_on(1, (2, 3))
+    back.forward((2, 3))
     back.close(1, (0, 1))
-    back.hop(0, (0, 1))
+    back.send(0, (0, 1))
 
     def gm_copy(e):
         return pltpu.make_async_copy(gst.at[e % 2], gm_h.at[e], gm_s.at[e % 2])
@@ -933,20 +929,17 @@
                 dw_copy(k, r, 1).start()
 
     turn(6, 12)
-    back.pass_on(1, (4, 5))
+    mem_grad(0, 2)
+    back.forward((4, 5))
     back.close(1, (2, 3))
-    back.hop(0, (2, 3))
-    back.pass_on(0, (0, 1))
-    mem_grad(0, 4)
+    back.send(0, (2, 3))
+    mem_grad(2, 8)
     back.close(1, (4, 5))
-    back.hop(0, (4, 5))
-    back.pass_on(0, (2, 3))
-    mem_grad(4, 8)
+    back.send(0, (4, 5))
     ring.close(0)
     sums = [pltpu.make_async_copy(accB.at[:, :, :, me["z"]], sumE, sum_s.at[0]), pltpu.make_async_copy(accC.at[me["z"]], sumF, sum_s.at[1])]
     for c in sums:
         c.start()
-    back.pass_on(0, (4, 5))
     weight_grad(0, 3)
     for n in range(6):
         dq_ref[:, 128 * n:128 * n + 128] = (0.125 * back.result(n)).T
@@ -970,9 +963,9 @@
         in_specs=[VS] * 3 + [HS] * 9, out_specs=(VS,) + (HS,) * 4, input_output_aliases={11: 2},
         scratch_shapes=[vm(6, 4, 4, 128, 128), vm(6, 4, 4, 128, 128), vf(4, 4, 24, 128), vm(768, 768), vm(768, 768),
                         vm(2, 4, 192, 256), vm(2, 4, 192, 256), vm(2, 4, 256, 192), vm(4, 256, 768), vm(768, 3072), vm(3072, 768), vm(3072, 768),
-                        vf(2, 384, 768), vm(2, 256, 768), vm(6, 4, 4, 128, 128), vm(6, 2, 2, 128, 128), vm(6, 2, 4, 128, 128), vm(6, 2, 128, 128), vm(6, 2, 128, 128),
-                        vm(2, 4, 4, 4, *bB), vm(4, 4, 4, *bC), vm(2, 4, 4, 4, *bB), vm(4, 4, 4, *bC), *stage_buffers(LEADS[:2], ((2,), bB), ((), bC)),
-                        DMA, DMA((3, 2, 4)), DMA((4,)), DMA((4,)), DMA((2,)), DMA((2, 2)), DMA((7, 2, 4)), DMA((7, 2, 4)), DMA((6, 2, 4)), DMA((6, 2, 4)),
+                        vf(2, 384, 768), vm(2, 256, 768), vm(6, 4, 4, 128, 128), *stage_buffers(LEAD_D, ((6,), (128, 128))),
+                        vm(2, 4, 4, 4, *bB), vm(4, 4, 4, *bC), vm(2, 4, 4, 4, *bB), vm(4, 4, 4, *bC), *stage_buffers(LEAD_A[:2], ((2,), bB), ((), bC)),
+                        DMA, DMA((3, 2, 4)), DMA((4,)), DMA((4,)), DMA((2,)), DMA((2, 2)), DMA((7, 2, 4)), DMA((7, 2, 4)), DMA((6, 2, 5)), DMA((6, 2, 5)),
                         DMA((3, 1, 4)), DMA((3, 1, 4)), DMA((3, 4)), DMA((3, 4)), DMA((3, 4)), DMA((2,))],
         compiler_params=pltpu.CompilerParams(collective_id=3, has_side_effects=True, vmem_limit_bytes=60 << 20),
         name="cross_backward",

time: 296 us -> 282 us (0.953)
  Pallas kernels: 288 us -> 274 us
    pallas_call x1, Pallas kernels: 52.9 us -> 47.7 us  [gather(): pl.pallas_call(gather_kernel, out_shape=(SDS((4, 4, 4, 2, 3, 32, 384), BF...]
    pallas_call x1, Pallas kernels: 51.8 us -> 47.3 us  [scatter(): pl.pallas_call(scatter_kernel, out_shape=(SDS((6, 8, 768), F32), SDS((6,...]
    pallas_call x1, Pallas kernels: 82.5 us -> 78 us  [cross_bwd(): pl.pallas_call(cross_bwd_kernel, out_shape=(SDS((128, 768), F32), SDS((8,...]
where the time goes in v2:
time: 282 us; the launch traced here: 277 us
  Pallas kernels  274 us (97%)
    pallas_call x1, Pallas kernels, cross_bwd(): pl.pallas_call(cross_bwd_kernel, out_shape=(SDS((128, 768), F32), SDS((8,...  78 us
    pallas_call x1, Pallas kernels, cross_fwd(): pl.pallas_call(cross_fwd_kernel, out_shape=(SDS((6, 4, 4, 128, 128), BF),...  62.4 us
    pallas_call x1, Pallas kernels, gather(): pl.pallas_call(gather_kernel, out_shape=(SDS((4, 4, 4, 2, 3, 32, 384), BF...  47.7 us
    pallas_call x1, Pallas kernels, scatter(): pl.pallas_call(scatter_kernel, out_shape=(SDS((6, 8, 768), F32), SDS((6,...  47.3 us
    pallas_call x1, Pallas kernels, ffn(): pl.pallas_call(ffn_kernel, out_shape=(SDS((128, 768), BF), SDS((128, 768)...  16.3 us
    pallas_call x1, Pallas kernels, self_bwd(): pl.pallas_call(self_bwd_kernel, out_shape=(SDS((128, 768), F32), SDS((8,...  13.7 us
    pallas_call x1, Pallas kernels, self_fwd(): pl.pallas_call(self_fwd_kernel, out_shape=(row, row, SDS((3, 128, 768), B...  5.9 us

profile of v2, /device:TPU:0, one launch (start us, length us, event | category | flops | bytes accessed | tf_op | source)
XLA Modules:
  0.0 276.9 jit_solution(12908449880391630451)
XLA Ops:
  1.3 0.7 convert_convert_fusion
  2.0 0.2 dynamic_update_slice.6
  2.2 0.1 dynamic_update_slice.7.info
  2.3 0.0 copy-start
  2.3 0.6 copy-done
  2.9 47.7 %gather_attention_weights.1 = (bf16[4,4,4,2,3,32,384]{6,5,4,3,2,1,0:T(8,128)(2,1)}, bf16[4,4,4,2,2,48,256]{6,5,4,3,2,1,0:T(8,128)(2,1)}, bf16[4,2,4,4,16,768]{5,...) custom-call(f32[6,8,768]{2,1,0:T(8,128)} %bitcast.41, f32[6,2,2048]{2,1,0:T(2,128)} %bitcast.43, f32[16,768]{1,0:T(8,128)} %refs_8_.1, ...), custom_call_target="tpu_custom_call" | custom-call | tf_op jit(solution)/shard_map/gather_attention_weights/pallas_call | solution.py:420
  50.6 5.9 %self_forward.1 = (bf16[128,768]{1,0:T(8,128)(2,1)}, bf16[128,768]{1,0:T(8,128)(2,1)}, bf16[3,128,768]{2,1,0:T(8,128)(2,1)}, bf16[128,768]{1,0:T(8,128)(2,1)}, f...) custom-call(bf16[128,768]{1,0:T(8,128)(2,1)} %bitcast.39, f32[8,768]{1,0:T(8,128)} %get-tuple-element.76.gains, ...), custom_call_target="tpu_custom_call" | custom-call | tf_op jit(solution)/shard_map/self_forward/pallas_call | solution.py:1050
  56.5 62.4 %cross_forward.1 = (bf16[6,4,4,128,128]{4,3,2,1,0:T(8,128)(2,1)}, bf16[16,192,768]{2,1,0:T(8,128)(2,1)}, bf16[16,192,768]{2,1,0:T(8,128)(2,1)}, bf16[16,768,192]...) custom-call(bf16[128,768]{1,0:T(8,128)(2,1)} %get-tuple-element.79.q, ...), custom_call_target="tpu_custom_call", output_to_operand_aliasing={{4}: (4, {}), {5}: (5, {})} | custom-call | tf_op jit(solution)/shard_map/cross_forward/pallas_call | solution.py:756
  118.9 16.3 %feed_forward.1 = (bf16[128,768]{1,0:T(8,128)(2,1)}, bf16[128,768]{1,0:T(8,128)(2,1)}, f32[24,128]{1,0:T(8,128)}, f32[128,768]{1,0:T(8,128)}, f32[1,768]{1,0:T(1...) custom-call(f32[128,768]{1,0:T(8,128)} %get-tuple-element.78.x1, ...), custom_call_target="tpu_custom_call" | custom-call | tf_op jit(solution)/shard_map/feed_forward/pallas_call | solution.py:1138
  135.2 78.0 %cross_backward.1 = (f32[128,768]{1,0:T(8,128)}, f32[8,384,768]{2,1,0:T(8,128)}, bf16[16,768,384]{2,1,0:T(8,128)(2,1)}, bf16[2,4,4,48,256]{4,3,2,1,0:T(8,128)(2,1)}, bf16[4,4,16,768]{3,2,1,0:T(8,128)(2,1)}) custom-call(bf16[128,768]{1,0:T(8,128)(2,1)} %get-tuple-element.88.do, f32[24,128]{1,0:T(8,128)} %get-tuple-element.89.st, ...), custom_call_target="tpu_custom_call", output_to_operand_aliasing={{2}: (11, {})} | custom-call | tf_op jit(solution)/shard_map/cross_backward/pallas_call | solution.py:960
  213.3 13.7 %self_backward.1 = (f32[128,768]{1,0:T(8,128)}, f32[8,8,128]{2,1,0:T(8,128)}, bf16[16,768,384]{2,1,0:T(8,128)(2,1)}, f32[16,192,768]{2,1,0:T(8,128)}) custom-call(f32[128,768]{1,0:T(8,128)} %get-tuple-element.97.dq2, bf16[128,768]{1,0:T(8,128)(2,1)} %get-tuple-element.98.h2, f32[128,768]{1,0:T(8,128)} %get-tuple-element.78.x1, ...), custom_call_target="tpu_custom_call", output_to_operand_aliasing={{2}: (12, {})} | custom-call | tf_op jit(solution)/shard_map/self_backward/pallas_call | solution.py:1237
  227.0 47.3 %scatter_attention_grads.1 = (f32[6,8,768]{2,1,0:T(8,128)}, f32[6,2,2048]{2,1,0:T(2,128)}, f32[16,768]{1,0:T(8,128)}, f32[8,128]{1,0:T(8,128)}) custom-call(bf16[4,4,4,2,3,32,384]{6,5,4,3,2,1,0:T(8,128)(2,1)} %bitcast.32, bf16[2,4,4,48,256]{4,3,2,1,0:T(8,128)(2,1)} %get-tuple-element.110.sumE, bf16[4,4,16,768]{3,2,1,0:T(8,128)(2,1)} %get-tuple-element.111.sumF, ...), custom_call_target="tpu_custom_call" | custom-call | tf_op jit(solution)/shard_map/scatter_attention_grads/pallas_call | solution.py:523
  274.3 2.5 adam.1
  (1 shorter events, 0.0 us)
Async XLA Ops:
  2.3 0.6 copy-start
